TPU v7x, 32 devices: a whole 2x2x4 slice. The times are simulated.
32 devices in a mesh: seq: 2 (over x), ep: 16 (over z, y, core).
Axes of the slice: x: 2, y: 2, z: 4, core: 2. Of those that a mesh axis runs over, the one named last changes fastest.
Arguments:
- tokens: bfloat16 [256, 7168], P(('seq', 'ep')), may hold values from -50 to 50
- out_grad: bfloat16 [256, 7168], P(('seq', 'ep')), may hold values from -6 to 6
- routes: int32 [256, 8], P(('seq', 'ep')), may hold values from 0 to 15, all different within a row; in each aligned block of 8 rows (0 to 7, 8 to 15, ...) at most 5 rows name the same one
- gate_fixed: int32 [256, 8], P(('seq', 'ep')), may hold values from 1 to 65535
- ramp_step: int32 [16], replicated, may hold values from 1 to 8
- norm_gain: float32 [7168], replicated, may hold values from 0.1 to 1.9
- w_gate: bfloat16 [16, 7168, 1024], P('ep', None, 'seq'), may hold values from -0.0625 to 0.0625
- w_up: bfloat16 [16, 7168, 1024], P('ep', None, 'seq'), may hold values from -0.0625 to 0.0625
- w_down: bfloat16 [16, 1024, 7168], P('ep', 'seq'), may hold values from -0.1875 to 0.1875
Outputs:
- mixed: bfloat16 [256, 7168], P(('seq', 'ep'))
- tokens_grad: bfloat16 [256, 7168], P(('seq', 'ep'))
- gain_grad: float32 [7168], P(('seq', 'ep'))
- w_gate_grad: bfloat16 [16, 7168, 1024], P('ep', None, 'seq')
- w_up_grad: bfloat16 [16, 7168, 1024], P('ep', None, 'seq')
- w_down_grad: bfloat16 [16, 1024, 7168], P('ep', 'seq')
Inputs may be any that keep to these rules, and one draw needn't show every extreme that they name: `routes`: each row names 8 different experts. Within the rows of one device (aligned blocks of 8 rows) no expert is named more than 5 times, and in some such block one expert is named exactly 5 times.
All inputs are finite; a program needn't handle non-finite values.
Results may differ from a plain program's by a relative error of at most 0.023.
Values may be sent and summed in bfloat16 or wider, within the bound.
No kernel may reach another device: no remote copies, remote signals or barrier semaphores. Data moves between devices by JAX's collectives and lax.ppermute only.
A program may use at most 128 MiB of HBM per device.

v0:
```python
import functools

import jax
import jax.numpy as jnp
from jax import lax
from jax.experimental import pallas as pl
from jax.experimental.pallas import tpu as pltpu
from jax.sharding import PartitionSpec as P


RAMP = 8
CORES = 2
DEPTH = 4

gate_unit = 65536.0
norm_eps = 1e-06
META = 128
CHUNK = 1024
WIDE = 1792
WHOLE_ROWS = 256
VMEM_MIB = 14


AXES = ("seq", "ep")


def contract_rows(left, right):
    return lax.dot_general(
        left, right, (((0,), (0,)), ((), ())), preferred_element_type=jnp.float32
    )


def contract_cols(left, right):
    return lax.dot_general(
        left, right, (((1,), (1,)), ((), ())), preferred_element_type=jnp.float32
    )


def matmul(left, right):
    return jnp.dot(left, right, preferred_element_type=jnp.float32)


class Torus:
    def __init__(self, seq_count, ep_count):
        self.nx = seq_count
        self.nc = CORES
        self.nz = DEPTH
        self.ny = ep_count // (CORES * DEPTH)
        self.count = seq_count * ep_count
        self.swap = self.nx == self.ny

    def place(self, i):
        core = i % self.nc
        y = i // self.nc % self.ny
        z = i // (self.nc * self.ny) % self.nz
        x = i // (self.nc * self.ny * self.nz)
        return [x, z, y, core]

    def index(self, x, z, y, core):
        return ((x * self.nz + z) * self.ny + y) * self.nc + core

    def axis(self, step, core):
        first = 0 if (self.swap and core == 1) else 2
        return (1, first, 2 - first, 3)[step]

    def size(self, step):
        return (self.nz, self.ny, self.nx, self.nc)[step]

    def pairs(self, step, shift):
        sizes = [self.nx, self.nz, self.ny, self.nc]
        found = []
        for i in range(self.count):
            spot = self.place(i)
            axis = self.axis(step, spot[3])
            spot[axis] ^= shift
            found.append((i, self.index(*spot)))
        return found

    def check(self):
        assert all(n & (n - 1) == 0 for n in (self.nx, self.ny, self.nz, self.nc))


def shift_rows(torus, rows, step, shift):
    return lax.ppermute(rows, AXES, torus.pairs(step, shift))


def planes(torus, rows):
    second = [rows] + [shift_rows(torus, rows, 1, s) for s in range(1, torus.size(1))]
    third = [second] + [
        [shift_rows(torus, piece, 2, s) for piece in second]
        for s in range(1, torus.size(2))
    ]
    return [piece for row in third for piece in row]


def gather(torus, rows):
    near = jnp.concatenate(planes(torus, rows), axis=0)
    near_pair = shift_rows(torus, near, 3, 1)
    others = [shift_rows(torus, rows, 0, s) for s in range(1, torus.nz)]
    far = planes(torus, jnp.concatenate(others, axis=0))
    far_pair = [shift_rows(torus, piece, 3, 1) for piece in far]
    return far + far_pair + [near, near_pair]


def load_rows(refs, cols):
    far, near = refs[:-2], refs[-2:]
    half = len(far) // CORES
    own = near[0].shape[0] // half
    found = []
    for core in range(CORES):
        block = near[core][:, cols].astype(jnp.float32)
        for k in range(half):
            wide = far[core * half + k][:, cols].astype(jnp.float32)
            found.append(jnp.concatenate([wide, block[k * own : (k + 1) * own]], axis=0))
    return found


def wide_sum(parts):
    total = parts[0].astype(jnp.float32)
    for part in parts[1:]:
        total = total + part.astype(jnp.float32)
    return total


def scatter_sum(torus, parts, after=None):
    n3, n2 = torus.size(2), torus.size(1)
    each = parts[0][0].shape[0] // n2
    got = [None] * n3
    for s3 in reversed(range(n3)):
        got[s3] = shift_rows(torus, parts[1][s3], 3, 1)
    near = [
        [
            [parts[0][s3][s2 * each : (s2 + 1) * each], got[s3][s2 * each : (s2 + 1) * each]]
            for s2 in range(n2)
        ]
        for s3 in range(n3)
    ]
    for s2 in reversed(range(n2)):
        for s3 in range(1, n3):
            send = wide_sum(near[s3][s2]).astype(jnp.bfloat16)
            near[0][s2].append(shift_rows(torus, send, 2, s3))
    for s2 in range(1, n2):
        send = wide_sum(near[0][s2]).astype(jnp.bfloat16)
        near[0][0].append(shift_rows(torus, send, 1, s2))
    if after is not None:
        near[0][0][-1], after = lax.optimization_barrier((near[0][0][-1], after))
    total = wide_sum(near[0][0])
    rows = each // torus.nz
    last = [total[each - rows :]]
    for shift in reversed(range(1, torus.nz)):
        block = total[(shift - 1) * rows : shift * rows].astype(jnp.bfloat16)
        last.append(shift_rows(torus, block, 0, shift))
    return wide_sum(last) if after is None else (wide_sum(last), after)


def gain_rows(span):
    return (span + 2 * META - 2) // META


def gain_tiles(torus, device, gain_ref, span, rows):
    count = gain_rows(span)
    core = device % CORES
    tiles = []
    for other in range(CORES):
        odd = (core + other) % CORES
        for s3 in range(torus.size(2)):
            for s2 in range(torus.size(1)):
                for sz in [*range(1, torus.nz), 0]:
                    even_mask = torus.index(s3, sz, s2, other)
                    odd_mask = torus.index(s2, sz, s3, other) if torus.swap else even_mask
                    target = device ^ jnp.where(odd == 1, odd_mask, even_mask)
                    value = gain_ref[pl.ds(target * span // META, count), :]
                    high = value.astype(jnp.bfloat16).astype(jnp.float32)
                    rest = jnp.zeros((rows - 2 * count, META), jnp.float32)
                    tiles.append(jnp.concatenate([high, value - high, rest], axis=0))
    return tiles


def gates_of(table, place, ramp_step, top):
    place = place.astype(jnp.int32)
    expert = place.astype(jnp.float32)
    ramp = ramp_step[place].astype(jnp.float32)
    gates = table[:, top : 2 * top] * 256.0 + table[:, 2 * top : 3 * top]
    coef = jnp.sum(jnp.where(table[:, :top] == expert, gates, 0.0), axis=1, keepdims=True)
    return coef / gate_unit * ramp / RAMP


def fold_lanes(rows):
    part = rows[:, :META]
    for c in range(1, rows.shape[1] // META):
        part = part + rows[:, c * META : (c + 1) * META]
    return part


def pack_kernel(tokens, routes, gates, out, meta):
    width = tokens.shape[1]
    top = routes.shape[1]
    out[:, :width] = tokens[...]
    fixed = gates[...]
    high = fixed // 256
    meta[...] = jnp.zeros_like(meta)
    meta[:, :top] = routes[...].astype(jnp.float32)
    meta[:, top : 2 * top] = high.astype(jnp.float32)
    meta[:, 2 * top : 3 * top] = (fixed - 256 * high).astype(jnp.float32)
    out[:, width:] = meta[...].astype(jnp.bfloat16)


def pack(tokens, routes, gates):
    rows, width = tokens.shape
    vmem = pl.BlockSpec(memory_space=pltpu.VMEM)
    return pl.pallas_call(
        pack_kernel,
        in_specs=[vmem] * 3,
        out_specs=vmem,
        out_shape=jax.ShapeDtypeStruct((rows, width + META), jnp.bfloat16),
        scratch_shapes=[pltpu.VMEM((rows, META), jnp.float32)],
        compiler_params=pltpu.CompilerParams(vmem_limit_bytes=4 * 2**20),
        name="pack",
    )(*off_chip(tokens, routes, gates))


def send_parts(rows, parts, cols, sems, first):
    size = parts[0].shape[0]
    copies = [
        pltpu.make_async_copy(
            rows.at[p * size : (p + 1) * size, cols], ref.at[:, cols], sems.at[first + p]
        )
        for p, ref in enumerate(parts)
    ]
    for copy in copies:
        copy.start()
    return copies


def forward_whole(*refs, pieces, width, top):
    spot, ramp_step = refs[:2]
    tok = refs[2 : 2 + pieces]
    gain, wg, wu, wd = refs[2 + pieces : 6 + pieces]
    outs = refs[6 + pieces :]
    scaled, pre_gate, pre_up, hidden, side = outs[:5]
    parts = outs[5:-4]
    acc_g, acc_u, sums, sems = outs[-4:]
    pending = []
    squares = []
    for k in range(width // WIDE):
        cols = slice(k * WIDE, (k + 1) * WIDE)
        g = gain[:, cols]
        for p, x in enumerate(load_rows(tok, cols)):
            each = x.shape[0]
            scaled[p * each : (p + 1) * each, cols] = (x * g).astype(jnp.bfloat16)
            part = fold_lanes(x * x)
            if k == 0:
                squares.append(part)
            else:
                squares[p] = squares[p] + part
        xs = scaled[:, cols]
        if k == 0:
            acc_g[...] = matmul(xs, wg[cols, :])
            acc_u[...] = matmul(xs, wu[cols, :])
        else:
            acc_g[...] += matmul(xs, wg[cols, :])
            acc_u[...] += matmul(xs, wu[cols, :])
    total = jnp.sum(jnp.concatenate(squares, axis=0), axis=1, keepdims=True)
    recip = lax.rsqrt(total / width + norm_eps)
    table = jnp.concatenate(load_rows(tok, slice(width, width + META)), axis=0)
    coef = gates_of(table, spot[0], ramp_step, top)
    pg = recip * acc_g[...]
    pu = recip * acc_u[...]
    pre_gate[...] = pg
    pre_up[...] = pu
    hidden[...] = (coef * (pg * jax.nn.sigmoid(pg) * pu)).astype(jnp.bfloat16)
    lane = lax.broadcasted_iota(jnp.int32, side.shape, 1)
    side[...] = jnp.where(lane == 0, recip, jnp.where(lane == 1, coef, 0.0))
    for k in range(width // WIDE):
        cols = slice(k * WIDE, (k + 1) * WIDE)
        sums[:, cols] = matmul(hidden[...], wd[:, cols]).astype(jnp.bfloat16)
        pending += send_parts(sums, parts, cols, sems, k * len(parts))
    for copy in pending:
        copy.wait()


def backward_whole(*refs, pieces, width, torus):
    spot = refs[0]
    grad = refs[1 : 1 + pieces]
    tok = refs[1 + pieces : 1 + 2 * pieces]
    wd, wg, wu, pre_gate, pre_up, side = refs[1 + 2 * pieces : 7 + 2 * pieces]
    outs = refs[7 + 2 * pieces :]
    og_all, pre_grads = outs[:2]
    parts = outs[2:-6]
    acc, gate_s, up_s, sums, gain_ref, sems = outs[-6:]
    pending = []
    steps = width // WIDE
    for k in range(steps):
        cols = slice(k * WIDE, (k + 1) * WIDE)
        for p, rows in enumerate(load_rows(grad, cols)):
            each = rows.shape[0]
            og_all[p * each : (p + 1) * each, cols] = rows.astype(jnp.bfloat16)
        got = contract_cols(og_all[:, cols], wd[:, cols])
        if k == 0:
            acc[...] = got
        else:
            acc[...] += got
    recip = side[:, 0:1]
    coef = side[:, 1:2]
    pre_grads_of(acc, pre_gate, pre_up, recip, coef, gate_s, up_s, pre_grads)
    gain_ref[...] = jnp.zeros_like(gain_ref)
    for k in range(steps):
        cols = slice(k * WIDE, (k + 1) * WIDE)
        back = contract_cols(gate_s[...], wg[cols, :]) + contract_cols(up_s[...], wu[cols, :])
        sums[:, cols] = back.astype(jnp.bfloat16)
        total = None
        for p, x in enumerate(load_rows(tok, cols)):
            each = x.shape[0]
            rows = slice(p * each, (p + 1) * each)
            part = back[rows] * (x * recip[rows])
            total = part if p == 0 else total + part
        keep_gain(gain_ref, total, k * WIDE // META)
        if k == steps - 1:
            sums[:, width:] = gain_block(torus, spot, gain_ref, width, recip.shape[0])
            cols = slice(k * WIDE, width + META)
        pending += send_parts(sums, parts, cols, sems, steps + k * len(parts))
    for copy in pending:
        copy.wait()


def keep_gain(gain_ref, total, first):
    row = jnp.sum(total, axis=0, keepdims=True)
    for c in range(row.shape[1] // META):
        gain_ref[first + c : first + c + 1, :] = row[:, c * META : (c + 1) * META]


def gain_block(torus, spot, gain_ref, width, rows):
    device = spot[1].astype(jnp.int32)
    tiles = gain_tiles(torus, device, gain_ref, width // torus.count, rows // torus.count)
    return jnp.concatenate(tiles, axis=0).astype(jnp.bfloat16)


def prefetch_kernel(_, *refs):
    count = len(refs) // 2
    sems = refs[-1]
    copies = [
        pltpu.make_async_copy(refs[k], refs[count + k], sems.at[k]) for k in range(count)
    ]
    for copy in copies:
        copy.start()
    for copy in copies:
        copy.wait()


def off_chip(*arrays):
    return [pltpu.with_memory_space_constraint(a, pltpu.HBM) for a in arrays]


def on_chip(*arrays):
    return [pltpu.with_memory_space_constraint(a, pltpu.VMEM) for a in arrays]


def prefetch(spot, weights):
    return pl.pallas_call(
        prefetch_kernel,
        in_specs=[pl.BlockSpec(memory_space=pltpu.SMEM)]
        + [pl.BlockSpec(memory_space=pltpu.HBM)] * len(weights),
        out_specs=[pl.BlockSpec(memory_space=pltpu.VMEM)] * len(weights),
        out_shape=[pltpu.VMEM(w.shape, w.dtype) for w in weights],
        scratch_shapes=[pltpu.SemaphoreType.DMA((len(weights),))],
        compiler_params=pltpu.CompilerParams(vmem_limit_bytes=2**20),
        name="prefetch",
    )(spot, *off_chip(*weights))


def pre_grads_of(acc, pre_gate, pre_up, recip, coef, gate_s, up_s, pre_grads):
    hidden_grad = coef * acc[...]
    pg = pre_gate[...]
    pu = pre_up[...]
    sigma = jax.nn.sigmoid(pg)
    gate_grad = hidden_grad * pu * sigma * (1.0 + pg * (1.0 - sigma))
    up_grad = hidden_grad * (pg * sigma)
    gate_s[...] = gate_grad.astype(jnp.bfloat16)
    up_s[...] = up_grad.astype(jnp.bfloat16)
    half = gate_grad.shape[1]
    pre_grads[:, :half] = (recip * gate_grad).astype(jnp.bfloat16)
    pre_grads[:, half:] = (recip * up_grad).astype(jnp.bfloat16)


def forward_kernel(*refs, pieces, steps, width, top):
    spot, ramp_step = refs[:2]
    tok = refs[2 : 2 + pieces]
    meta = refs[2 + pieces : 2 + 2 * pieces]
    gain, wg, wu, wd = refs[2 + 2 * pieces : 6 + 2 * pieces]
    outs = refs[6 + 2 * pieces :]
    scaled, pre_gate, pre_up, hidden, side = outs[:5]
    parts = outs[5:-3]
    acc_g, acc_u, squares = outs[-3:]
    i = pl.program_id(0)

    @pl.when(i < steps)
    def _():
        g = gain[...]
        for p, x in enumerate(load_rows(tok, slice(None))):
            each = x.shape[0]
            part_rows = slice(p * each, (p + 1) * each)
            scaled[part_rows, :] = (x * g).astype(jnp.bfloat16)
            part = fold_lanes(x * x)
            squares[part_rows, :] = jnp.where(i == 0, part, squares[part_rows, :] + part)
        xs = scaled[...]
        got_g = matmul(xs, wg[...])
        got_u = matmul(xs, wu[...])

        @pl.when(i == 0)
        def _():
            acc_g[...] = got_g
            acc_u[...] = got_u

        @pl.when(i > 0)
        def _():
            acc_g[...] += got_g
            acc_u[...] += got_u

    @pl.when(i == steps - 1)
    def _():
        recip = lax.rsqrt(jnp.sum(squares[...], axis=1, keepdims=True) / width + norm_eps)
        table = jnp.concatenate(load_rows(meta, slice(None)), axis=0)
        coef = gates_of(table, spot[0], ramp_step, top)
        pg = recip * acc_g[...]
        pu = recip * acc_u[...]
        pre_gate[...] = pg
        pre_up[...] = pu
        hidden[...] = (coef * (pg * jax.nn.sigmoid(pg) * pu)).astype(jnp.bfloat16)
        lane = lax.broadcasted_iota(jnp.int32, side.shape, 1)
        side[...] = jnp.where(lane == 0, recip, jnp.where(lane == 1, coef, 0.0))

    @pl.when(i >= steps)
    def _():
        out = matmul(hidden[...], wd[...]).astype(jnp.bfloat16)
        size = parts[0].shape[0]
        for p, ref in enumerate(parts):
            ref[...] = out[p * size : (p + 1) * size]


def backward_kernel(*refs, pieces, steps, width, torus):
    spot = refs[0]
    grad = refs[1 : 1 + pieces]
    tok = refs[1 + pieces : 1 + 2 * pieces]
    wd, wg, wu, pre_gate, pre_up, side = refs[1 + 2 * pieces : 7 + 2 * pieces]
    outs = refs[7 + 2 * pieces :]
    og_all, pre_grads = outs[:2]
    parts = outs[2:-4]
    acc, gate_s, up_s, gain_ref = outs[-4:]
    i = pl.program_id(0)
    size = parts[0].shape[0]

    @pl.when(i < steps)
    def _():
        for p, rows in enumerate(load_rows(grad, slice(None))):
            each = rows.shape[0]
            og_all[p * each : (p + 1) * each, :] = rows.astype(jnp.bfloat16)
        got = contract_cols(og_all[...], wd[...])

        @pl.when(i == 0)
        def _():
            acc[...] = got
            gain_ref[...] = jnp.zeros_like(gain_ref)

        @pl.when(i > 0)
        def _():
            acc[...] += got

    @pl.when(i == steps - 1)
    def _():
        recip = side[:, 0:1]
        coef = side[:, 1:2]
        pre_grads_of(acc, pre_gate, pre_up, recip, coef, gate_s, up_s, pre_grads)

    for k in range(steps):

        @pl.when(i == steps + k)
        def _(k=k):
            back = contract_cols(gate_s[...], wg[...]) + contract_cols(up_s[...], wu[...])
            recip = side[:, 0:1]
            total = None
            for p, x in enumerate(load_rows(tok, slice(None))):
                each = x.shape[0]
                rows = slice(p * each, (p + 1) * each)
                part = back[rows] * (x * recip[rows])
                total = part if p == 0 else total + part
            keep_gain(gain_ref, total, k * CHUNK // META)
            out = back.astype(jnp.bfloat16)
            for p, ref in enumerate(parts):
                ref[...] = out[p * size : (p + 1) * size]

    @pl.when(i == 2 * steps)
    def _():
        out = gain_block(torus, spot, gain_ref, width, side.shape[0])
        for p, ref in enumerate(parts):
            ref[:, :META] = out[p * size : (p + 1) * size]


def up_grads_kernel(scaled, pre_grads, wg_grad, wu_grad):
    both = contract_rows(scaled[...], pre_grads[...]).astype(jnp.bfloat16)
    half = wg_grad.shape[1]
    wg_grad[...] = both[:, :half]
    wu_grad[...] = both[:, half:]


def down_grad_kernel(hidden, og_all, wd_grad):
    wd_grad[...] = contract_rows(hidden[...], og_all[...]).astype(jnp.bfloat16)


def params(mib=56):
    return pltpu.CompilerParams(dimension_semantics=("arbitrary",), vmem_limit_bytes=mib * 2**20)


def placed(shapes, low, high):
    return [
        (pltpu.VMEM if low <= k < high else pltpu.HBM)(s.shape, s.dtype)
        for k, s in enumerate(shapes)
    ]


def shapes_of(rows, width, hid, size, parts):
    scratch = [
        jax.ShapeDtypeStruct((rows, width), jnp.bfloat16),
        jax.ShapeDtypeStruct((rows, hid), jnp.float32),
        jax.ShapeDtypeStruct((rows, hid), jnp.float32),
        jax.ShapeDtypeStruct((rows, hid), jnp.bfloat16),
        jax.ShapeDtypeStruct((rows, META), jnp.float32),
    ]
    return scratch + [jax.ShapeDtypeStruct((size, width), jnp.bfloat16)] * parts


def cost(flops, size):
    return pl.CostEstimate(flops=int(flops), bytes_accessed=int(size), transcendentals=0)


def forward(torus, tok, gain, wg, wu, wd, spot, ramp_step, top):
    width, hid = wg.shape
    steps = width // CHUNK
    pieces = len(tok)
    heights = [t.shape[0] for t in tok]
    rows = sum(heights)
    n3 = torus.size(2)
    size = rows // (CORES * n3)
    first = lambda i: jnp.minimum(i, steps - 1)
    later = lambda i: jnp.maximum(i - steps, 0)
    fixed = lambda i: (0, 0)
    if rows <= WHOLE_ROWS:
        vmem = pl.BlockSpec(memory_space=pltpu.VMEM)
        hbm = pl.BlockSpec(memory_space=pltpu.HBM)
        outs = pl.pallas_call(
            functools.partial(forward_whole, pieces=pieces, width=width, top=top),
            in_specs=[pl.BlockSpec(memory_space=pltpu.SMEM)] * 2 + [vmem] * (pieces + 4),
            out_specs=[vmem] * 5 + [hbm] * (CORES * n3),
            out_shape=placed(shapes_of(rows, width, hid, size, CORES * n3), 0, 5),
            scratch_shapes=[
                pltpu.VMEM((rows, hid), jnp.float32),
                pltpu.VMEM((rows, hid), jnp.float32),
                pltpu.VMEM((rows, width), jnp.bfloat16),
                pltpu.SemaphoreType.DMA((width // WIDE * (1 + CORES * n3),)),
            ],
            compiler_params=pltpu.CompilerParams(vmem_limit_bytes=VMEM_MIB * 2**20),
            cost_estimate=cost(6 * rows * width * hid, 6 * width * hid + 6 * rows * width),
            name="forward",
        )(spot, ramp_step, *tok, gain, *on_chip(wg, wu, wd))
        return (*outs[:5], [outs[5 + c * n3 : 5 + (c + 1) * n3] for c in range(CORES)])
    outs = pl.pallas_call(
        functools.partial(forward_kernel, pieces=pieces, steps=steps, width=width, top=top),
        grid=(2 * steps,),
        in_specs=[pl.BlockSpec(memory_space=pltpu.SMEM)] * 2
        + [pl.BlockSpec((h, CHUNK), lambda i: (0, first(i))) for h in heights]
        + [pl.BlockSpec((h, META), lambda i: (0, width // META)) for h in heights]
        + [
            pl.BlockSpec((1, CHUNK), lambda i: (0, first(i))),
            pl.BlockSpec((CHUNK, hid), lambda i: (first(i), 0)),
            pl.BlockSpec((CHUNK, hid), lambda i: (first(i), 0)),
            pl.BlockSpec((hid, CHUNK), lambda i: (0, later(i))),
        ],
        out_specs=[
            pl.BlockSpec((rows, CHUNK), lambda i: (0, first(i))),
            pl.BlockSpec((rows, hid), fixed),
            pl.BlockSpec((rows, hid), fixed),
            pl.BlockSpec((rows, hid), fixed),
            pl.BlockSpec((rows, META), fixed),
        ]
        + [pl.BlockSpec((size, CHUNK), lambda i: (0, later(i)))] * (CORES * n3),
        out_shape=shapes_of(rows, width, hid, size, CORES * n3),
        scratch_shapes=[
            pltpu.VMEM((rows, hid), jnp.float32),
            pltpu.VMEM((rows, hid), jnp.float32),
            pltpu.VMEM((rows, META), jnp.float32),
        ],
        compiler_params=params(),
        cost_estimate=cost(6 * rows * width * hid, 6 * width * hid + 6 * rows * width),
        name="forward",
    )(spot, ramp_step, *tok, *tok, gain, wg, wu, wd)
    scaled, pre_gate, pre_up, hidden, side = outs[:5]
    parts = [outs[5 + c * n3 : 5 + (c + 1) * n3] for c in range(CORES)]
    return scaled, pre_gate, pre_up, hidden, side, parts


def backward(torus, spot, grad, tok, wd, wg, wu, pre_gate, pre_up, side):
    width, hid = wg.shape
    steps = width // CHUNK
    pieces = len(grad)
    heights = [g.shape[0] for g in grad]
    rows = sum(heights)
    n3 = torus.size(2)
    size = rows // (CORES * n3)
    first = lambda i: jnp.minimum(i, steps - 1)
    later = lambda i: jnp.maximum(i - steps, 0)
    held = lambda i: jnp.clip(i - steps, 0, steps - 1)
    fixed = lambda i: (0, 0)
    shapes = [
        jax.ShapeDtypeStruct((rows, width), jnp.bfloat16),
        jax.ShapeDtypeStruct((rows, 2 * hid), jnp.bfloat16),
    ] + [jax.ShapeDtypeStruct((size, width + META), jnp.bfloat16)] * (CORES * n3)
    if rows <= WHOLE_ROWS:
        vmem = pl.BlockSpec(memory_space=pltpu.VMEM)
        hbm = pl.BlockSpec(memory_space=pltpu.HBM)
        outs = pl.pallas_call(
            functools.partial(backward_whole, pieces=pieces, width=width, torus=torus),
            in_specs=[pl.BlockSpec(memory_space=pltpu.SMEM)] + [vmem] * (2 * pieces + 6),
            out_specs=[vmem, vmem] + [hbm] * (CORES * n3),
            out_shape=placed(shapes, 0, 2),
            scratch_shapes=[
                pltpu.VMEM((rows, hid), jnp.float32),
                pltpu.VMEM((rows, hid), jnp.bfloat16),
                pltpu.VMEM((rows, hid), jnp.bfloat16),
                pltpu.VMEM((rows, width + META), jnp.bfloat16),
                pltpu.VMEM((width // META + 8, META), jnp.float32),
                pltpu.SemaphoreType.DMA((width // WIDE * (1 + CORES * n3),)),
            ],
            compiler_params=pltpu.CompilerParams(vmem_limit_bytes=VMEM_MIB * 2**20),
            cost_estimate=cost(6 * rows * width * hid, 6 * width * hid + 6 * rows * width),
            name="backward",
        )(spot, *grad, *tok, *on_chip(wd, wg, wu, pre_gate, pre_up, side))
        return (*outs[:2], [outs[2 + c * n3 : 2 + (c + 1) * n3] for c in range(CORES)])
    outs = pl.pallas_call(
        functools.partial(backward_kernel, pieces=pieces, steps=steps, width=width, torus=torus),
        grid=(2 * steps + 1,),
        in_specs=[pl.BlockSpec(memory_space=pltpu.SMEM)]
        + [pl.BlockSpec((h, CHUNK), lambda i: (0, first(i))) for h in heights]
        + [pl.BlockSpec((h, CHUNK), lambda i: (0, held(i))) for h in heights]
        + [
            pl.BlockSpec((hid, CHUNK), lambda i: (0, first(i))),
            pl.BlockSpec((CHUNK, hid), lambda i: (held(i), 0)),
            pl.BlockSpec((CHUNK, hid), lambda i: (held(i), 0)),
            pl.BlockSpec((rows, hid), fixed),
            pl.BlockSpec((rows, hid), fixed),
            pl.BlockSpec((rows, META), fixed),
        ],
        out_specs=[
            pl.BlockSpec((rows, CHUNK), lambda i: (0, first(i))),
            pl.BlockSpec((rows, 2 * hid), fixed),
        ]
        + [pl.BlockSpec((size, CHUNK), lambda i: (0, later(i)))] * (CORES * n3),
        out_shape=shapes,
        scratch_shapes=[
            pltpu.VMEM((rows, hid), jnp.float32),
            pltpu.VMEM((rows, hid), jnp.bfloat16),
            pltpu.VMEM((rows, hid), jnp.bfloat16),
            pltpu.VMEM((width // META + 8, META), jnp.float32),
        ],
        compiler_params=params(),
        cost_estimate=cost(6 * rows * width * hid, 6 * width * hid + 6 * rows * width),
        name="backward",
    )(spot, *grad, *tok, wd, wg, wu, pre_gate, pre_up, side)
    parts = [outs[2 + c * n3 : 2 + (c + 1) * n3] for c in range(CORES)]
    return outs[0], outs[1], parts


def up_grads(scaled, pre_grads):
    rows, width = scaled.shape
    hid = pre_grads.shape[1] // 2
    step = WIDE if rows <= WHOLE_ROWS else CHUNK
    return pl.pallas_call(
        up_grads_kernel,
        grid=(width // step,),
        in_specs=[
            pl.BlockSpec((rows, step), lambda i: (0, i)),
            pl.BlockSpec((rows, 2 * hid), lambda i: (0, 0)),
        ],
        out_specs=[pl.BlockSpec((step, hid), lambda i: (i, 0))] * 2,
        out_shape=[jax.ShapeDtypeStruct((width, hid), jnp.bfloat16)] * 2,
        compiler_params=params(20),
        cost_estimate=cost(4 * rows * width * hid, 4 * width * hid + 2 * rows * width),
        name="up_grads",
    )(*(on_chip(scaled, pre_grads) if rows <= WHOLE_ROWS else (scaled, pre_grads)))


def down_grad(hidden, og_all):
    rows, width = og_all.shape
    hid = hidden.shape[1]
    step = WIDE if rows <= WHOLE_ROWS else CHUNK
    return pl.pallas_call(
        down_grad_kernel,
        grid=(width // step,),
        in_specs=[
            pl.BlockSpec((rows, hid), lambda i: (0, 0)),
            pl.BlockSpec((rows, step), lambda i: (0, i)),
        ],
        out_specs=pl.BlockSpec((hid, step), lambda i: (0, i)),
        out_shape=jax.ShapeDtypeStruct((hid, width), jnp.bfloat16),
        compiler_params=params(20),
        cost_estimate=cost(2 * rows * width * hid, 2 * width * hid + 2 * rows * width),
        name="down_grad",
    )(*(on_chip(hidden, og_all) if rows <= WHOLE_ROWS else (hidden, og_all)))


def layer(tokens, out_grad, routes, gate_fixed, ramp_step, norm_gain, w_gate, w_up, w_down):
    seq_count = lax.axis_size("seq")
    ep_count = lax.axis_size("ep")
    torus = Torus(seq_count, ep_count)
    torus.check()
    width = tokens.shape[1]
    top = routes.shape[1]
    tok = gather(torus, pack(tokens, routes, gate_fixed))
    grad = gather(torus, out_grad)
    expert = lax.axis_index("ep")
    span = width // torus.count
    device = lax.axis_index("seq") * ep_count + expert
    start = (device * span % META).astype(jnp.uint32)
    spot = jnp.stack([expert.astype(jnp.uint32), device.astype(jnp.uint32), start])
    gain = norm_gain[None, :]
    wg, wu, wd = w_gate[0], w_up[0], w_down[0]
    if tokens.shape[0] * seq_count * ep_count <= WHOLE_ROWS:
        held = []
        for weight in (wg, wu, wd):
            held += prefetch(spot, [weight])
        wg, wu, wd = held
    scaled, pre_gate, pre_up, hidden, side, out_parts = forward(
        torus, tok, gain, wg, wu, wd, spot, ramp_step, top
    )
    og_all, pre_grads, parts = backward(torus, spot, grad, tok, wd, wg, wu, pre_gate, pre_up, side)
    w_gate_grad, w_up_grad = up_grads(scaled, pre_grads)
    mixed, w_gate_grad = scatter_sum(torus, out_parts, w_gate_grad)
    mixed = mixed.astype(jnp.bfloat16)
    total = scatter_sum(torus, parts)
    normed_grad = total[:, :width]
    count = gain_rows(span)
    gain_part = total[:count, width:] + total[count : 2 * count, width:]
    gain_grad = lax.dynamic_slice(gain_part.reshape(-1), (start,), (span,))
    w_down_grad = down_grad(hidden, og_all)[None]
    own = tokens.astype(jnp.float32)
    own_recip = lax.rsqrt(jnp.mean(own * own, axis=1, keepdims=True) + norm_eps)
    weighted = gain * normed_grad
    inner = jnp.sum(weighted * own, axis=1, keepdims=True)
    tokens_grad = (
        own_recip * weighted - own * own_recip * own_recip * own_recip * inner / width
    ).astype(jnp.bfloat16)
    return (mixed, tokens_grad, gain_grad, w_gate_grad[None], w_up_grad[None], w_down_grad)


def solution(mesh):
    return jax.shard_map(
        layer,
        mesh=mesh,
        in_specs=(
            P(("seq", "ep"), None),
            P(("seq", "ep"), None),
            P(("seq", "ep"), None),
            P(("seq", "ep"), None),
            P(),
            P(),
            P("ep", None, "seq"),
            P("ep", None, "seq"),
            P("ep", "seq", None),
        ),
        out_specs=(
            P(("seq", "ep"), None),
            P(("seq", "ep"), None),
            P(("seq", "ep")),
            P("ep", None, "seq"),
            P("ep", None, "seq"),
            P("ep", "seq", None),
        ),
        check_vma=False,
    )
```

profile of v0, /device:TPU:0, one launch (start us, length us, event | category | flops | bytes accessed | tf_op | source)
XLA Modules:
  0.0 152.8 jit_solution(1011080602703295571)
XLA Ops:
  1.6 3.1 %collective-permute-start = (bf16[8,7296]{1,0:T(8,128)(2,1)S(1)}, bf16[8,7296]{1,0:T(8,128)(2,1)S(1)}, u32[]{:S(2)}, u32[]{:S(2)}) collective-permute-start(bf16[8,7296]{1,0:T(8,128)(2,1)S(1)} %pack.1), channel_id=1, source_target_pairs={{0,4},{1,5},{2,6},{3,7},{4,0},{5,1},{6,2},{7,3},{8,12},{9,13},{10,... | collective-permute-start | bytes 350216 | tf_op jit(solution)/shard_map/ppermute | solution.py:84
  4.7 2.6 %collective-permute-start.1 = (bf16[8,7296]{1,0:T(8,128)(2,1)S(1)}, bf16[8,7296]{1,0:T(8,128)(2,1)S(1)}, u32[]{:S(2)}, u32[]{:S(2)}) collective-permute-start(bf16[8,7296]{1,0:T(8,128)(2,1)S(1)} %pack.1), channel_id=1, source_target_pairs={{0,8},{1,9},{2,10},{3,11},{4,12},{5,13},{6,14},{7,15},{8,0},{9,1},... | collective-permute-start | bytes 350216 | tf_op jit(solution)/shard_map/ppermute | solution.py:84
  7.3 1.7 %collective-permute-start.10 = (bf16[8,7296]{1,0:T(8,128)(2,1)S(1)}, bf16[8,7296]{1,0:T(8,128)(2,1)S(1)}, u32[]{:S(2)}, u32[]{:S(2)}) collective-permute-start(bf16[8,7296]{1,0:T(8,128)(2,1)S(1)} %pack.1), channel_id=1, source_target_pairs={{0,2},{1,17},{2,0},{3,19},{4,6},{5,21},{6,4},{7,23},{8,10},{9,25},... | collective-permute-start | bytes 350216 | tf_op jit(solution)/shard_map/ppermute | solution.py:84
  10.7 3.6 %prefetch.3.refs_13_.refs_22_ = bf16[7168,512]{1,0:T(8,128)(2,1)S(1)} custom-call(u32[3]{0:T(128)S(1)} %pad_add_fusion._.refs_0_, bf16[7168,512]{1,0:T(8,128)(2,1)} %bitcast.13), custom_call_target="tpu_custom_call" | custom-call | tf_op jit(solution)/shard_map/prefetch/pallas_call | solution.py:359
  14.4 3.6 %prefetch.4.refs_14_.refs_23_ = bf16[7168,512]{1,0:T(8,128)(2,1)S(1)} custom-call(u32[3]{0:T(128)S(1)} %pad_add_fusion._.refs_0_, bf16[7168,512]{1,0:T(8,128)(2,1)} %bitcast.14), custom_call_target="tpu_custom_call" | custom-call | tf_op jit(solution)/shard_map/prefetch/pallas_call | solution.py:359
  18.0 3.6 %prefetch.5.refs_15_.refs_21_ = bf16[512,7168]{1,0:T(8,128)(2,1)S(1)} custom-call(u32[3]{0:T(128)S(1)} %pad_add_fusion._.refs_0_, bf16[512,7168]{1,0:T(8,128)(2,1)} %bitcast.15), custom_call_target="tpu_custom_call" | custom-call | tf_op jit(solution)/shard_map/prefetch/pallas_call | solution.py:359
  21.7 3.6 %collective-permute-start.20 = (bf16[8,7168]{1,0:T(8,128)(2,1)S(1)}, bf16[8,7168]{1,0:T(8,128)(2,1)S(1)}, u32[]{:S(2)}, u32[]{:S(2)}) collective-permute-start(bf16[8,7168]{1,0:T(8,128)(2,1)S(1)} %copy-done.7), channel_id=1, source_target_pairs={{0,8},{1,9},{2,10},{3,11},{4,12},{5,13},{6,14},{7,15},{8,0},{9,1},... | collective-permute-start | bytes 344072 | tf_op jit(solution)/shard_map/ppermute | solution.py:84
  25.3 4.5 %collective-permute-done.20 = bf16[8,7168]{1,0:T(8,128)(2,1)S(1)} collective-permute-done((bf16[8,7168]{1,0:T(8,128)(2,1)S(1)}, bf16[8,7168]{1,0:T(8,128)(2,1)S(1)}, u32[]{:S(2)}, u32[]{:S(2)}) %collective-permute-start.20) | collective-permute-done | bytes 114720 | tf_op jit(solution)/shard_map/ppermute | solution.py:84
  30.6 5.7 %collective-permute-done.21 = bf16[8,7168]{1,0:T(8,128)(2,1)S(1)} collective-permute-done((bf16[8,7168]{1,0:T(8,128)(2,1)S(1)}, bf16[8,7168]{1,0:T(8,128)(2,1)S(1)}, u32[]{:S(2)}, u32[]{:S(2)}) %collective-permute-start.21) | collective-permute-done | bytes 114720 | tf_op jit(solution)/shard_map/ppermute | solution.py:84
  37.8 3.3 %collective-permute-done.29 = bf16[8,7168]{1,0:T(8,128)(2,1)S(1)} collective-permute-done((bf16[8,7168]{1,0:T(8,128)(2,1)S(1)}, bf16[8,7168]{1,0:T(8,128)(2,1)S(1)}, u32[]{:S(2)}, u32[]{:S(2)}) %collective-permute-start.29) | collective-permute-done | bytes 114720 | tf_op jit(solution)/shard_map/ppermute | solution.py:84
  41.1 3.2 %collective-permute-start.11 = (bf16[8,7296]{1,0:T(8,128)(2,1)S(1)}, bf16[8,7296]{1,0:T(8,128)(2,1)S(1)}, u32[]{:S(2)}, u32[]{:S(2)}) collective-permute-start(bf16[8,7296]{1,0:T(8,128)(2,1)S(1)} %pack.1), channel_id=1, source_target_pairs={{0,16},{1,3},{2,18},{3,1},{4,20},{5,7},{6,22},{7,5},{8,24},{9,11},... | collective-permute-start | bytes 350216 | tf_op jit(solution)/shard_map/ppermute | solution.py:84
  44.8 1.7 %collective-permute-start.31 = (bf16[8,7168]{1,0:T(8,128)(2,1)S(1)}, bf16[8,7168]{1,0:T(8,128)(2,1)S(1)}, u32[]{:S(2)}, u32[]{:S(2)}) collective-permute-start(bf16[8,7168]{1,0:T(8,128)(2,1)S(1)} %collective-permute-done.29), channel_id=1, source_target_pairs={{0,16},{1,3},{2,18},{3,1},{4,20},{5,7},{6,22},{7,5},{8,24},{9,11},... | collective-permute-start | bytes 344072 | tf_op jit(solution)/shard_map/ppermute | solution.py:84
  46.6 4.2 %collective-permute-done.30 = bf16[8,7168]{1,0:T(8,128)(2,1)S(1)} collective-permute-done((bf16[8,7168]{1,0:T(8,128)(2,1)S(1)}, bf16[8,7168]{1,0:T(8,128)(2,1)S(1)}, u32[]{:S(2)}, u32[]{:S(2)}) %collective-permute-start.30) | collective-permute-done | bytes 114720 | tf_op jit(solution)/shard_map/ppermute | solution.py:84
  53.2 2.0 %collective-permute-start.4 = (bf16[24,7296]{1,0:T(8,128)(2,1)S(1)}, bf16[24,7296]{1,0:T(8,128)(2,1)S(1)}, u32[]{:S(2)}, u32[]{:S(2)}) collective-permute-start(bf16[24,7296]{1,0:T(8,128)(2,1)S(1)} %constant_dynamic-update-slice_fusion.refs_2_.refs_11_), channel_id=1, source_target_pairs={{0,16},{1,3},{2,18},{3,1},{4,20},{5,7},{6,22},{7,5},{8,24},{9,11},... | collective-permute-start | bytes 1050632 | tf_op jit(solution)/shard_map/ppermute | solution.py:84
  55.9 7.0 %collective-permute-done.3.refs_3_.refs_12_ = bf16[24,7296]{1,0:T(8,128)(2,1)S(1)} collective-permute-done((bf16[24,7296]{1,0:T(8,128)(2,1)S(1)}, bf16[24,7296]{1,0:T(8,128)(2,1)S(1)}, u32[]{:S(2)}, u32[]{:S(2)}) %collective-permute-start.3) | collective-permute-done | bytes 350240 | tf_op jit(solution)/shard_map/ppermute | solution.py:84
  62.9 2.0 %collective-permute-start.5 = (bf16[24,7296]{1,0:T(8,128)(2,1)S(1)}, bf16[24,7296]{1,0:T(8,128)(2,1)S(1)}, u32[]{:S(2)}, u32[]{:S(2)}) collective-permute-start(bf16[24,7296]{1,0:T(8,128)(2,1)S(1)} %collective-permute-done.3.refs_3_.refs_12_), channel_id=1, source_target_pairs={{0,16},{1,3},{2,18},{3,1},{4,20},{5,7},{6,22},{7,5},{8,24},{9,11},... | collective-permute-start | bytes 1050632 | tf_op jit(solution)/shard_map/ppermute | solution.py:84
  65.7 4.5 %collective-permute-done.5.refs_5_.refs_14_ = bf16[24,7296]{1,0:T(8,128)(2,1)S(1)} collective-permute-done((bf16[24,7296]{1,0:T(8,128)(2,1)S(1)}, bf16[24,7296]{1,0:T(8,128)(2,1)S(1)}, u32[]{:S(2)}, u32[]{:S(2)}) %collective-permute-start.5) | collective-permute-done | bytes 350240 | tf_op jit(solution)/shard_map/ppermute | solution.py:84
  70.8 3.1 %collective-permute-done.24.refs_4_ = bf16[24,7168]{1,0:T(8,128)(2,1)S(1)} collective-permute-done((bf16[24,7168]{1,0:T(8,128)(2,1)S(1)}, bf16[24,7168]{1,0:T(8,128)(2,1)S(1)}, u32[]{:S(2)}, u32[]{:S(2)}) %collective-permute-start.24) | collective-permute-done | bytes 344096 | tf_op jit(solution)/shard_map/ppermute | solution.py:84
  74.9 8.2 %forward.1 = (bf16[256,7168]{1,0:T(8,128)(2,1)S(1)}, f32[256,512]{1,0:T(8,128)S(1)}, f32[256,512]{1,0:T(8,128)S(1)}, bf16[256,512]{1,0:T(8,128)(2,1)S(1)}, f32[2...) custom-call(u32[3]{0:T(128)S(1)} %pad_add_fusion._.refs_0_, ...), custom_call_target="tpu_custom_call" | custom-call | flops 5637144576 | bytes 33030144 | tf_op jit(solution)/shard_map/forward/pallas_call | solution.py:549
  83.8 8.5 %backward.1 = (bf16[256,7168]{1,0:T(8,128)(2,1)S(1)}, bf16[256,1024]{1,0:T(8,128)(2,1)S(1)}, bf16[64,7296]{1,0:T(8,128)(2,1)}, bf16[64,7296]{1,0:T(8,128)(2,1)},...) custom-call(u32[3]{0:T(128)S(1)} %pad_add_fusion._.refs_0_, ...), custom_call_target="tpu_custom_call" | custom-call | flops 5637144576 | bytes 33030144 | tf_op jit(solution)/shard_map/backward/pallas_call | solution.py:619
  92.8 4.7 %down_grad.1 = bf16[512,7168]{1,0:T(8,128)(2,1)} custom-call(bf16[256,512]{1,0:T(8,128)(2,1)S(1)} %get-tuple-element.42.hidden, bf16[256,7168]{1,0:T(8,128)(2,1)S(1)} %get-tuple-element.43.og_all), custom_call_target="tpu_custom_call" | custom-call | flops 1879048192 | bytes 11010048 | tf_op jit(solution)/shard_map/down_grad/pallas_call | solution.py:694
  97.5 6.4 %up_grads.1 = (bf16[7168,512]{1,0:T(8,128)(2,1)}, bf16[7168,512]{1,0:T(8,128)(2,1)}) custom-call(bf16[256,7168]{1,0:T(8,128)(2,1)S(1)} %get-tuple-element.29.scaled, bf16[256,1024]{1,0:T(8,128)(2,1)S(1)} %get-tuple-element.33.pre_grads), custom_call_target="tpu_custom_call" | custom-call | flops 3758096384 | bytes 18350080 | tf_op jit(solution)/shard_map/up_grads/pallas_call | solution.py:675
  104.1 2.1 %collective-permute-start.17 = (bf16[32,7168]{1,0:T(8,128)(2,1)S(1)}, bf16[32,7168]{1,0:T(8,128)(2,1)S(1)}, u32[]{:S(2)}, u32[]{:S(2)}) collective-permute-start(bf16[32,7168]{1,0:T(8,128)(2,1)S(1)} %get-tuple-element.53), channel_id=1, source_target_pairs={{0,16},{1,3},{2,18},{3,1},{4,20},{5,7},{6,22},{7,5},{8,24},{9,11},... | collective-permute-start | bytes 1376264 | tf_op jit(solution)/shard_map/ppermute | solution.py:84
  106.5 2.0 %collective-permute-start.39 = (bf16[32,7296]{1,0:T(8,128)(2,1)S(1)}, bf16[32,7296]{1,0:T(8,128)(2,1)S(1)}, u32[]{:S(2)}, u32[]{:S(2)}) collective-permute-start(bf16[32,7296]{1,0:T(8,128)(2,1)S(1)} %get-tuple-element.51), channel_id=1, source_target_pairs={{0,16},{1,3},{2,18},{3,1},{4,20},{5,7},{6,22},{7,5},{8,24},{9,11},... | collective-permute-start | bytes 1400840 | tf_op jit(solution)/shard_map/ppermute | solution.py:84
  108.6 4.1 %collective-permute-done.17 = bf16[32,7168]{1,0:T(8,128)(2,1)S(1)} collective-permute-done((bf16[32,7168]{1,0:T(8,128)(2,1)S(1)}, bf16[32,7168]{1,0:T(8,128)(2,1)S(1)}, u32[]{:S(2)}, u32[]{:S(2)}) %collective-permute-start.17) | collective-permute-done | bytes 458784 | tf_op jit(solution)/shard_map/ppermute | solution.py:84
  113.3 14.2 %collective-permute-done.39 = bf16[32,7296]{1,0:T(8,128)(2,1)S(1)} collective-permute-done((bf16[32,7296]{1,0:T(8,128)(2,1)S(1)}, bf16[32,7296]{1,0:T(8,128)(2,1)S(1)}, u32[]{:S(2)}, u32[]{:S(2)}) %collective-permute-start.39) | collective-permute-done | bytes 466976 | tf_op jit(solution)/shard_map/ppermute | solution.py:84
  128.5 3.9 %collective-permute-start.34 = (bf16[8,7168]{1,0:T(8,128)(2,1)S(1)}, bf16[8,7168]{1,0:T(8,128)(2,1)S(1)}, u32[]{:S(2)}, u32[]{:S(2)}) collective-permute-start(bf16[8,7168]{1,0:T(8,128)(2,1)S(1)} %get-tuple-element.59), channel_id=1, source_target_pairs={{0,8},{1,9},{2,10},{3,11},{4,12},{5,13},{6,14},{7,15},{8,0},{9,1},... | collective-permute-start | bytes 344072 | tf_op jit(solution)/shard_map/ppermute | solution.py:84
  132.9 2.3 %collective-permute-done.38 = bf16[32,7296]{1,0:T(8,128)(2,1)S(1)} collective-permute-done((bf16[32,7296]{1,0:T(8,128)(2,1)S(1)}, bf16[32,7296]{1,0:T(8,128)(2,1)S(1)}, u32[]{:S(2)}, u32[]{:S(2)}) %collective-permute-start.38) | collective-permute-done | bytes 466976 | tf_op jit(solution)/shard_map/ppermute | solution.py:84
  137.0 2.5 %collective-permute-start.42 = (bf16[8,7296]{1,0:T(8,128)(2,1)S(1)}, bf16[8,7296]{1,0:T(8,128)(2,1)S(1)}, u32[]{:S(2)}, u32[]{:S(2)}) collective-permute-start(bf16[8,7296]{1,0:T(8,128)(2,1)S(1)} %get-tuple-element.56), channel_id=1, source_target_pairs={{0,8},{1,9},{2,10},{3,11},{4,12},{5,13},{6,14},{7,15},{8,0},{9,1},... | collective-permute-start | bytes 350216 | tf_op jit(solution)/shard_map/ppermute | solution.py:84
  139.5 1.9 %collective-permute-start.41 = (bf16[8,7296]{1,0:T(8,128)(2,1)S(1)}, bf16[8,7296]{1,0:T(8,128)(2,1)S(1)}, u32[]{:S(2)}, u32[]{:S(2)}) collective-permute-start(bf16[8,7296]{1,0:T(8,128)(2,1)S(1)} %get-tuple-element.54), channel_id=1, source_target_pairs={{0,12},{1,13},{2,14},{3,15},{4,8},{5,9},{6,10},{7,11},{8,4},{9,5},... | collective-permute-start | bytes 350216 | tf_op jit(solution)/shard_map/ppermute | solution.py:84
  142.1 2.2 %collective-permute-done.43 = bf16[8,7296]{1,0:T(8,128)(2,1)S(1)} collective-permute-done((bf16[8,7296]{1,0:T(8,128)(2,1)S(1)}, bf16[8,7296]{1,0:T(8,128)(2,1)S(1)}, u32[]{:S(2)}, u32[]{:S(2)}) %collective-permute-start.43) | collective-permute-done | bytes 116768 | tf_op jit(solution)/shard_map/ppermute | solution.py:84
  144.2 6.8 %collective-permute-done.42 = bf16[8,7296]{1,0:T(8,128)(2,1)S(1)} collective-permute-done((bf16[8,7296]{1,0:T(8,128)(2,1)S(1)}, bf16[8,7296]{1,0:T(8,128)(2,1)S(1)}, u32[]{:S(2)}, u32[]{:S(2)}) %collective-permute-start.42) | collective-permute-done | bytes 116768 | tf_op jit(solution)/shard_map/ppermute | solution.py:84
  (107 shorter events, 19.3 us)
Async XLA Ops:
  1.6 42.6 %collective-permute-start = (bf16[8,7296]{1,0:T(8,128)(2,1)S(1)}, bf16[8,7296]{1,0:T(8,128)(2,1)S(1)}, u32[]{:S(2)}, u32[]{:S(2)}) collective-permute-start(bf16[8,7296]{1,0:T(8,128)(2,1)S(1)} %pack.1), channel_id=1, source_target_pairs={{0,4},{1,5},{2,6},{3,7},{4,0},{5,1},{6,2},{7,3},{8,12},{9,13},{10,... | collective-permute-start | bytes 350216 | tf_op jit(solution)/shard_map/ppermute | solution.py:84
  4.7 39.7 %collective-permute-start.1 = (bf16[8,7296]{1,0:T(8,128)(2,1)S(1)}, bf16[8,7296]{1,0:T(8,128)(2,1)S(1)}, u32[]{:S(2)}, u32[]{:S(2)}) collective-permute-start(bf16[8,7296]{1,0:T(8,128)(2,1)S(1)} %pack.1), channel_id=1, source_target_pairs={{0,8},{1,9},{2,10},{3,11},{4,12},{5,13},{6,14},{7,15},{8,0},{9,1},... | collective-permute-start | bytes 350216 | tf_op jit(solution)/shard_map/ppermute | solution.py:84
  7.3 37.5 %collective-permute-start.2 = (bf16[8,7296]{1,0:T(8,128)(2,1)S(1)}, bf16[8,7296]{1,0:T(8,128)(2,1)S(1)}, u32[]{:S(2)}, u32[]{:S(2)}) collective-permute-start(bf16[8,7296]{1,0:T(8,128)(2,1)S(1)} %pack.1), channel_id=1, source_target_pairs={{0,12},{1,13},{2,14},{3,15},{4,8},{5,9},{6,10},{7,11},{8,4},{9,5},... | collective-permute-start | bytes 350216 | tf_op jit(solution)/shard_map/ppermute | solution.py:84
  7.3 43.8 %collective-permute-start.10 = (bf16[8,7296]{1,0:T(8,128)(2,1)S(1)}, bf16[8,7296]{1,0:T(8,128)(2,1)S(1)}, u32[]{:S(2)}, u32[]{:S(2)}) collective-permute-start(bf16[8,7296]{1,0:T(8,128)(2,1)S(1)} %pack.1), channel_id=1, source_target_pairs={{0,2},{1,17},{2,0},{3,19},{4,6},{5,21},{6,4},{7,23},{8,10},{9,25},... | collective-permute-start | bytes 350216 | tf_op jit(solution)/shard_map/ppermute | solution.py:84
  9.0 12.7 %collective-permute-start.19 = (bf16[8,7168]{1,0:T(8,128)(2,1)}, bf16[8,7168]{1,0:T(8,128)(2,1)S(1)}, u32[]{:S(2)}, u32[]{:S(2)}) collective-permute-start(bf16[8,7168]{1,0:T(8,128)(2,1)} %param.10), channel_id=1, source_target_pairs={{0,4},{1,5},{2,6},{3,7},{4,0},{5,1},{6,2},{7,3},{8,12},{9,13},{10,... | collective-permute-start | bytes 344072 | tf_op jit(solution)/shard_map/ppermute | solution.py:84
  41.1 11.7 %collective-permute-start.11 = (bf16[8,7296]{1,0:T(8,128)(2,1)S(1)}, bf16[8,7296]{1,0:T(8,128)(2,1)S(1)}, u32[]{:S(2)}, u32[]{:S(2)}) collective-permute-start(bf16[8,7296]{1,0:T(8,128)(2,1)S(1)} %pack.1), channel_id=1, source_target_pairs={{0,16},{1,3},{2,18},{3,1},{4,20},{5,7},{6,22},{7,5},{8,24},{9,11},... | collective-permute-start | bytes 350216 | tf_op jit(solution)/shard_map/ppermute | solution.py:84
  44.4 20.6 %collective-permute-start.22 = (bf16[24,7168]{1,0:T(8,128)(2,1)S(1)}, bf16[24,7168]{1,0:T(8,128)(2,1)S(1)}, u32[]{:S(2)}, u32[]{:S(2)}) collective-permute-start(bf16[24,7168]{1,0:T(8,128)(2,1)S(1)} %constant_dynamic-update-slice_fusion.3.refs_1_), channel_id=1, source_target_pairs={{0,2},{1,17},{2,0},{3,19},{4,6},{5,21},{6,4},{7,23},{8,10},{9,25},... | collective-permute-start | bytes 1032200 | tf_op jit(solution)/shard_map/ppermute | solution.py:84
  50.8 12.1 %collective-permute-start.3 = (bf16[24,7296]{1,0:T(8,128)(2,1)S(1)}, bf16[24,7296]{1,0:T(8,128)(2,1)S(1)}, u32[]{:S(2)}, u32[]{:S(2)}) collective-permute-start(bf16[24,7296]{1,0:T(8,128)(2,1)S(1)} %constant_dynamic-update-slice_fusion.refs_2_.refs_11_), channel_id=1, source_target_pairs={{0,2},{1,17},{2,0},{3,19},{4,6},{5,21},{6,4},{7,23},{8,10},{9,25},... | collective-permute-start | bytes 1050632 | tf_op jit(solution)/shard_map/ppermute | solution.py:84
  52.8 12.3 %collective-permute-start.23 = (bf16[24,7168]{1,0:T(8,128)(2,1)S(1)}, bf16[24,7168]{1,0:T(8,128)(2,1)S(1)}, u32[]{:S(2)}, u32[]{:S(2)}) collective-permute-start(bf16[24,7168]{1,0:T(8,128)(2,1)S(1)} %constant_dynamic-update-slice_fusion.3.refs_1_), channel_id=1, source_target_pairs={{0,16},{1,3},{2,18},{3,1},{4,20},{5,7},{6,22},{7,5},{8,24},{9,11},... | collective-permute-start | bytes 1032200 | tf_op jit(solution)/shard_map/ppermute | solution.py:84
  53.2 11.9 %collective-permute-start.4 = (bf16[24,7296]{1,0:T(8,128)(2,1)S(1)}, bf16[24,7296]{1,0:T(8,128)(2,1)S(1)}, u32[]{:S(2)}, u32[]{:S(2)}) collective-permute-start(bf16[24,7296]{1,0:T(8,128)(2,1)S(1)} %constant_dynamic-update-slice_fusion.refs_2_.refs_11_), channel_id=1, source_target_pairs={{0,16},{1,3},{2,18},{3,1},{4,20},{5,7},{6,22},{7,5},{8,24},{9,11},... | collective-permute-start | bytes 1050632 | tf_op jit(solution)/shard_map/ppermute | solution.py:84
  55.9 9.7 %collective-permute-start.6 = (bf16[24,7296]{1,0:T(8,128)(2,1)S(1)}, bf16[24,7296]{1,0:T(8,128)(2,1)S(1)}, u32[]{:S(2)}, u32[]{:S(2)}) collective-permute-start(bf16[24,7296]{1,0:T(8,128)(2,1)S(1)} %constant_dynamic-update-slice_fusion.refs_2_.refs_11_), channel_id=1, source_target_pairs={{0,1},{1,0},{2,3},{3,2},{4,5},{5,4},{6,7},{7,6},{8,9},{9,8},{10,11... | collective-permute-start | bytes 1050632 | tf_op jit(solution)/shard_map/ppermute | solution.py:84
  65.0 8.9 %collective-permute-start.24 = (bf16[24,7168]{1,0:T(8,128)(2,1)S(1)}, bf16[24,7168]{1,0:T(8,128)(2,1)S(1)}, u32[]{:S(2)}, u32[]{:S(2)}) collective-permute-start(bf16[24,7168]{1,0:T(8,128)(2,1)S(1)} %collective-permute-done.22.refs_2_), channel_id=1, source_target_pairs={{0,16},{1,3},{2,18},{3,1},{4,20},{5,7},{6,22},{7,5},{8,24},{9,11},... | collective-permute-start | bytes 1032200 | tf_op jit(solution)/shard_map/ppermute | solution.py:84
  65.6 8.8 %collective-permute-start.8 = (bf16[24,7296]{1,0:T(8,128)(2,1)S(1)}, bf16[24,7296]{1,0:T(8,128)(2,1)S(1)}, u32[]{:S(2)}, u32[]{:S(2)}) collective-permute-start(bf16[24,7296]{1,0:T(8,128)(2,1)S(1)} %collective-permute-done.4.refs_4_.refs_13_), channel_id=1, source_target_pairs={{0,1},{1,0},{2,3},{3,2},{4,5},{5,4},{6,7},{7,6},{8,9},{9,8},{10,11... | collective-permute-start | bytes 1050632 | tf_op jit(solution)/shard_map/ppermute | solution.py:84
  70.2 12.9 %collective-permute-start.25 = (bf16[24,7168]{1,0:T(8,128)(2,1)S(1)}, bf16[24,7168]{1,0:T(8,128)(2,1)S(1)}, u32[]{:S(2)}, u32[]{:S(2)}) collective-permute-start(bf16[24,7168]{1,0:T(8,128)(2,1)S(1)} %constant_dynamic-update-slice_fusion.3.refs_1_), channel_id=1, source_target_pairs={{0,1},{1,0},{2,3},{3,2},{4,5},{5,4},{6,7},{7,6},{8,9},{9,8},{10,11... | collective-permute-start | bytes 1032200 | tf_op jit(solution)/shard_map/ppermute | solution.py:84
  73.9 9.4 %collective-permute-start.32 = (bf16[32,7168]{1,0:T(8,128)(2,1)S(1)}, bf16[32,7168]{1,0:T(8,128)(2,1)S(1)}, u32[]{:S(2)}, u32[]{:S(2)}) collective-permute-start(bf16[32,7168]{1,0:T(8,128)(2,1)S(1)} %constant_dynamic-update-slice_fusion.6.refs_9_), channel_id=1, source_target_pairs={{0,1},{1,0},{2,3},{3,2},{4,5},{5,4},{6,7},{7,6},{8,9},{9,8},{10,11... | collective-permute-start | bytes 1376264 | tf_op jit(solution)/shard_map/ppermute | solution.py:84
  73.9 9.9 %collective-permute-start.26 = (bf16[24,7168]{1,0:T(8,128)(2,1)S(1)}, bf16[24,7168]{1,0:T(8,128)(2,1)S(1)}, u32[]{:S(2)}, u32[]{:S(2)}) collective-permute-start(bf16[24,7168]{1,0:T(8,128)(2,1)S(1)} %collective-permute-done.22.refs_2_), channel_id=1, source_target_pairs={{0,1},{1,0},{2,3},{3,2},{4,5},{5,4},{6,7},{7,6},{8,9},{9,8},{10,11... | collective-permute-start | bytes 1032200 | tf_op jit(solution)/shard_map/ppermute | solution.py:84
  74.4 9.3 %collective-permute-start.27 = (bf16[24,7168]{1,0:T(8,128)(2,1)S(1)}, bf16[24,7168]{1,0:T(8,128)(2,1)S(1)}, u32[]{:S(2)}, u32[]{:S(2)}) collective-permute-start(bf16[24,7168]{1,0:T(8,128)(2,1)S(1)} %collective-permute-done.23.refs_3_), channel_id=1, source_target_pairs={{0,1},{1,0},{2,3},{3,2},{4,5},{5,4},{6,7},{7,6},{8,9},{9,8},{10,11... | collective-permute-start | bytes 1032200 | tf_op jit(solution)/shard_map/ppermute | solution.py:84
  74.5 9.3 %collective-permute-start.28 = (bf16[24,7168]{1,0:T(8,128)(2,1)S(1)}, bf16[24,7168]{1,0:T(8,128)(2,1)S(1)}, u32[]{:S(2)}, u32[]{:S(2)}) collective-permute-start(bf16[24,7168]{1,0:T(8,128)(2,1)S(1)} %collective-permute-done.24.refs_4_), channel_id=1, source_target_pairs={{0,1},{1,0},{2,3},{3,2},{4,5},{5,4},{6,7},{7,6},{8,9},{9,8},{10,11... | collective-permute-start | bytes 1032200 | tf_op jit(solution)/shard_map/ppermute | solution.py:84
  83.2 20.7 %collective-permute-start.15 = (bf16[64,7168]{1,0:T(8,128)(2,1)}, bf16[64,7168]{1,0:T(8,128)(2,1)S(1)}, u32[]{:S(2)}, u32[]{:S(2)}) collective-permute-start(bf16[64,7168]{1,0:T(8,128)(2,1)} %get-tuple-element.28), channel_id=1, source_target_pairs={{0,1},{1,0},{2,3},{3,2},{4,5},{5,4},{6,7},{7,6},{8,9},{9,8},{10,11... | collective-permute-start | bytes 2752520 | tf_op jit(solution)/shard_map/ppermute | solution.py:84
  83.3 25.2 %collective-permute-start.14 = (bf16[64,7168]{1,0:T(8,128)(2,1)}, bf16[64,7168]{1,0:T(8,128)(2,1)S(1)}, u32[]{:S(2)}, u32[]{:S(2)}) collective-permute-start(bf16[64,7168]{1,0:T(8,128)(2,1)} %get-tuple-element.26), channel_id=1, source_target_pairs={{0,1},{1,0},{2,3},{3,2},{4,5},{5,4},{6,7},{7,6},{8,9},{9,8},{10,11... | collective-permute-start | bytes 2752520 | tf_op jit(solution)/shard_map/ppermute | solution.py:84
  92.2 14.1 %collective-permute-start.37 = (bf16[64,7296]{1,0:T(8,128)(2,1)}, bf16[64,7296]{1,0:T(8,128)(2,1)S(1)}, u32[]{:S(2)}, u32[]{:S(2)}) collective-permute-start(bf16[64,7296]{1,0:T(8,128)(2,1)} %get-tuple-element.39), channel_id=1, source_target_pairs={{0,1},{1,0},{2,3},{3,2},{4,5},{5,4},{6,7},{7,6},{8,9},{9,8},{10,11... | collective-permute-start | bytes 2801672 | tf_op jit(solution)/shard_map/ppermute | solution.py:84
  92.4 20.9 %collective-permute-start.36 = (bf16[64,7296]{1,0:T(8,128)(2,1)}, bf16[64,7296]{1,0:T(8,128)(2,1)S(1)}, u32[]{:S(2)}, u32[]{:S(2)}) collective-permute-start(bf16[64,7296]{1,0:T(8,128)(2,1)} %get-tuple-element.37), channel_id=1, source_target_pairs={{0,1},{1,0},{2,3},{3,2},{4,5},{5,4},{6,7},{7,6},{8,9},{9,8},{10,11... | collective-permute-start | bytes 2801672 | tf_op jit(solution)/shard_map/ppermute | solution.py:84
  106.2 21.9 %collective-permute-start.16 = (bf16[32,7168]{1,0:T(8,128)(2,1)S(1)}, bf16[32,7168]{1,0:T(8,128)(2,1)S(1)}, u32[]{:S(2)}, u32[]{:S(2)}) collective-permute-start(bf16[32,7168]{1,0:T(8,128)(2,1)S(1)} %get-tuple-element.52), channel_id=1, source_target_pairs={{0,16},{1,3},{2,18},{3,1},{4,20},{5,7},{6,22},{7,5},{8,24},{9,11},... | collective-permute-start | bytes 1376264 | tf_op jit(solution)/shard_map/ppermute | solution.py:84
  106.5 21.0 %collective-permute-start.39 = (bf16[32,7296]{1,0:T(8,128)(2,1)S(1)}, bf16[32,7296]{1,0:T(8,128)(2,1)S(1)}, u32[]{:S(2)}, u32[]{:S(2)}) collective-permute-start(bf16[32,7296]{1,0:T(8,128)(2,1)S(1)} %get-tuple-element.51), channel_id=1, source_target_pairs={{0,16},{1,3},{2,18},{3,1},{4,20},{5,7},{6,22},{7,5},{8,24},{9,11},... | collective-permute-start | bytes 1400840 | tf_op jit(solution)/shard_map/ppermute | solution.py:84
  108.5 26.6 %collective-permute-start.38 = (bf16[32,7296]{1,0:T(8,128)(2,1)S(1)}, bf16[32,7296]{1,0:T(8,128)(2,1)S(1)}, u32[]{:S(2)}, u32[]{:S(2)}) collective-permute-start(bf16[32,7296]{1,0:T(8,128)(2,1)S(1)} %get-tuple-element.50), channel_id=1, source_target_pairs={{0,16},{1,3},{2,18},{3,1},{4,20},{5,7},{6,22},{7,5},{8,24},{9,11},... | collective-permute-start | bytes 1400840 | tf_op jit(solution)/shard_map/ppermute | solution.py:84
  112.8 15.3 %collective-permute-start.18 = (bf16[32,7168]{1,0:T(8,128)(2,1)S(1)}, bf16[32,7168]{1,0:T(8,128)(2,1)S(1)}, u32[]{:S(2)}, u32[]{:S(2)}) collective-permute-start(bf16[32,7168]{1,0:T(8,128)(2,1)S(1)} %add_convert_fusion.3), channel_id=1, source_target_pairs={{0,2},{1,17},{2,0},{3,19},{4,6},{5,21},{6,4},{7,23},{8,10},{9,25},... | collective-permute-start | bytes 1376264 | tf_op jit(solution)/shard_map/ppermute | solution.py:84
  127.7 8.9 %collective-permute-start.40 = (bf16[32,7296]{1,0:T(8,128)(2,1)S(1)}, bf16[32,7296]{1,0:T(8,128)(2,1)S(1)}, u32[]{:S(2)}, u32[]{:S(2)}) collective-permute-start(bf16[32,7296]{1,0:T(8,128)(2,1)S(1)} %add_convert_fusion), channel_id=1, source_target_pairs={{0,2},{1,17},{2,0},{3,19},{4,6},{5,21},{6,4},{7,23},{8,10},{9,25},... | collective-permute-start | bytes 1400840 | tf_op jit(solution)/shard_map/ppermute | solution.py:84
  128.4 11.1 %collective-permute-start.35 = (bf16[8,7168]{1,0:T(8,128)(2,1)S(1)}, bf16[8,7168]{1,0:T(8,128)(2,1)S(1)}, u32[]{:S(2)}, u32[]{:S(2)}) collective-permute-start(bf16[8,7168]{1,0:T(8,128)(2,1)S(1)} %get-tuple-element.58), channel_id=1, source_target_pairs={{0,4},{1,5},{2,6},{3,7},{4,0},{5,1},{6,2},{7,3},{8,12},{9,13},{10,... | collective-permute-start | bytes 344072 | tf_op jit(solution)/shard_map/ppermute | solution.py:84
  128.5 12.9 %collective-permute-start.34 = (bf16[8,7168]{1,0:T(8,128)(2,1)S(1)}, bf16[8,7168]{1,0:T(8,128)(2,1)S(1)}, u32[]{:S(2)}, u32[]{:S(2)}) collective-permute-start(bf16[8,7168]{1,0:T(8,128)(2,1)S(1)} %get-tuple-element.59), channel_id=1, source_target_pairs={{0,8},{1,9},{2,10},{3,11},{4,12},{5,13},{6,14},{7,15},{8,0},{9,1},... | collective-permute-start | bytes 344072 | tf_op jit(solution)/shard_map/ppermute | solution.py:84
  132.4 9.0 %collective-permute-start.33 = (bf16[8,7168]{1,0:T(8,128)(2,1)S(1)}, bf16[8,7168]{1,0:T(8,128)(2,1)S(1)}, u32[]{:S(2)}, u32[]{:S(2)}) collective-permute-start(bf16[8,7168]{1,0:T(8,128)(2,1)S(1)} %get-tuple-element.57), channel_id=1, source_target_pairs={{0,12},{1,13},{2,14},{3,15},{4,8},{5,9},{6,10},{7,11},{8,4},{9,5},... | collective-permute-start | bytes 344072 | tf_op jit(solution)/shard_map/ppermute | solution.py:84
  137.0 14.1 %collective-permute-start.42 = (bf16[8,7296]{1,0:T(8,128)(2,1)S(1)}, bf16[8,7296]{1,0:T(8,128)(2,1)S(1)}, u32[]{:S(2)}, u32[]{:S(2)}) collective-permute-start(bf16[8,7296]{1,0:T(8,128)(2,1)S(1)} %get-tuple-element.56), channel_id=1, source_target_pairs={{0,8},{1,9},{2,10},{3,11},{4,12},{5,13},{6,14},{7,15},{8,0},{9,1},... | collective-permute-start | bytes 350216 | tf_op jit(solution)/shard_map/ppermute | solution.py:84
  139.5 11.6 %collective-permute-start.41 = (bf16[8,7296]{1,0:T(8,128)(2,1)S(1)}, bf16[8,7296]{1,0:T(8,128)(2,1)S(1)}, u32[]{:S(2)}, u32[]{:S(2)}) collective-permute-start(bf16[8,7296]{1,0:T(8,128)(2,1)S(1)} %get-tuple-element.54), channel_id=1, source_target_pairs={{0,12},{1,13},{2,14},{3,15},{4,8},{5,9},{6,10},{7,11},{8,4},{9,5},... | collective-permute-start | bytes 350216 | tf_op jit(solution)/shard_map/ppermute | solution.py:84
  (20 other events, 303.3 us)
where the time goes:
time: 153 us
  waiting for transfers between devices  64.1 us (42%)
  starting transfers between devices  43.2 us (28%)
  Pallas kernels  39.6 us (26%)
  other arithmetic  3.18 us (2%)
  local copies, waits for them, and re-layouts  1.76 us (1%)
    ppermute x44, waiting for transfers between devices, shift_rows(): return lax.ppermute(rows, AXES, torus.pairs(step, shift))  64.1 us
    ppermute x44, starting transfers between devices, shift_rows(): return lax.ppermute(rows, AXES, torus.pairs(step, shift))  43.2 us
    pallas_call x3, Pallas kernels, prefetch(): pl.pallas_call(prefetch_kernel, in_specs=[pl.BlockSpec(memory_space=pltpu...  10.9 us
    pallas_call x1, Pallas kernels, backward(): pl.pallas_call(functools.partial(backward_whole, pieces=pieces, width=wid...  8.45 us
    pallas_call x1, Pallas kernels, forward(): pl.pallas_call(functools.partial(forward_whole, pieces=pieces, width=widt...  8.22 us
    pallas_call x1, Pallas kernels, up_grads(): pl.pallas_call(up_grads_kernel, grid=(width // step,), in_specs=[pl.Block...  6.36 us
    pallas_call x1, Pallas kernels, down_grad(): pl.pallas_call(down_grad_kernel, grid=(width // step,), in_specs=[pl.Bloc...  4.71 us
  transfers between devices with their start and end apart: 44, of which 14 were waited for; matrix products, arithmetic and copies ran while one was open for 2% of the time, Pallas kernels for 25%

commit v1 on v0

--- a/solution.py
+++ b/solution.py
@@ -18,7 +18,6 @@
 CHUNK = 1024
 WIDE = 1792
 WHOLE_ROWS = 256
-VMEM_MIB = 14
 
 
 AXES = ("seq", "ep")
@@ -97,9 +96,30 @@
     near = jnp.concatenate(planes(torus, rows), axis=0)
     near_pair = shift_rows(torus, near, 3, 1)
     others = [shift_rows(torus, rows, 0, s) for s in range(1, torus.nz)]
-    far = planes(torus, jnp.concatenate(others, axis=0))
+    line = join(others)
+    far = planes(torus, line)
     far_pair = [shift_rows(torus, piece, 3, 1) for piece in far]
     return far + far_pair + [near, near_pair]
+
+
+def join_kernel(*refs):
+    out = refs[-1]
+    each = refs[0].shape[0]
+    for k, ref in enumerate(refs[:-1]):
+        out[k * each : (k + 1) * each, :] = ref[...]
+
+
+def join(blocks):
+    rows, width = blocks[0].shape
+    vmem = pl.BlockSpec(memory_space=pltpu.VMEM)
+    return pl.pallas_call(
+        join_kernel,
+        in_specs=[vmem] * len(blocks),
+        out_specs=vmem,
+        out_shape=jax.ShapeDtypeStruct((rows * len(blocks), width), blocks[0].dtype),
+        compiler_params=limit(4),
+        name="join",
+    )(*blocks)
 
 
 def load_rows(refs, cols):
@@ -235,12 +255,9 @@
 def forward_whole(*refs, pieces, width, top):
     spot, ramp_step = refs[:2]
     tok = refs[2 : 2 + pieces]
-    gain, wg, wu, wd = refs[2 + pieces : 6 + pieces]
-    outs = refs[6 + pieces :]
-    scaled, pre_gate, pre_up, hidden, side = outs[:5]
-    parts = outs[5:-4]
-    acc_g, acc_u, sums, sems = outs[-4:]
-    pending = []
+    gain, wg, wu = refs[2 + pieces : 5 + pieces]
+    outs = refs[5 + pieces :]
+    scaled, pre_gate, pre_up, hidden, side, acc_g, acc_u = outs
     squares = []
     for k in range(width // WIDE):
         cols = slice(k * WIDE, (k + 1) * WIDE)
@@ -271,7 +288,13 @@
     hidden[...] = (coef * (pg * jax.nn.sigmoid(pg) * pu)).astype(jnp.bfloat16)
     lane = lax.broadcasted_iota(jnp.int32, side.shape, 1)
     side[...] = jnp.where(lane == 0, recip, jnp.where(lane == 1, coef, 0.0))
-    for k in range(width // WIDE):
+
+
+def out_whole(hidden, wd, *refs):
+    parts = refs[:-2]
+    sums, sems = refs[-2:]
+    pending = []
+    for k in range(wd.shape[1] // WIDE):
         cols = slice(k * WIDE, (k + 1) * WIDE)
         sums[:, cols] = matmul(hidden[...], wd[:, cols]).astype(jnp.bfloat16)
         pending += send_parts(sums, parts, cols, sems, k * len(parts))
@@ -528,6 +551,10 @@
     return scratch + [jax.ShapeDtypeStruct((size, width), jnp.bfloat16)] * parts
 
 
+def limit(mib):
+    return pltpu.CompilerParams(vmem_limit_bytes=mib * 2**20)
+
+
 def cost(flops, size):
     return pl.CostEstimate(flops=int(flops), bytes_accessed=int(size), transcendentals=0)
 
@@ -546,22 +573,31 @@
     if rows <= WHOLE_ROWS:
         vmem = pl.BlockSpec(memory_space=pltpu.VMEM)
         hbm = pl.BlockSpec(memory_space=pltpu.HBM)
+        shapes = shapes_of(rows, width, hid, size, CORES * n3)
         outs = pl.pallas_call(
             functools.partial(forward_whole, pieces=pieces, width=width, top=top),
-            in_specs=[pl.BlockSpec(memory_space=pltpu.SMEM)] * 2 + [vmem] * (pieces + 4),
-            out_specs=[vmem] * 5 + [hbm] * (CORES * n3),
-            out_shape=placed(shapes_of(rows, width, hid, size, CORES * n3), 0, 5),
+            in_specs=[pl.BlockSpec(memory_space=pltpu.SMEM)] * 2 + [vmem] * (pieces + 3),
+            out_specs=[vmem] * 5,
+            out_shape=placed(shapes[:5], 0, 5),
+            scratch_shapes=[pltpu.VMEM((rows, hid), jnp.float32)] * 2,
+            compiler_params=limit(8),
+            cost_estimate=cost(4 * rows * width * hid, 4 * width * hid + 4 * rows * width),
+            name="forward",
+        )(spot, ramp_step, *tok, gain, *on_chip(wg, wu))
+        parts = pl.pallas_call(
+            out_whole,
+            in_specs=[vmem] * 2,
+            out_specs=[hbm] * (CORES * n3),
+            out_shape=placed(shapes[5:], 0, 0),
             scratch_shapes=[
-                pltpu.VMEM((rows, hid), jnp.float32),
-                pltpu.VMEM((rows, hid), jnp.float32),
                 pltpu.VMEM((rows, width), jnp.bfloat16),
-                pltpu.SemaphoreType.DMA((width // WIDE * (1 + CORES * n3),)),
+                pltpu.SemaphoreType.DMA((width // WIDE * CORES * n3,)),
             ],
-            compiler_params=pltpu.CompilerParams(vmem_limit_bytes=VMEM_MIB * 2**20),
-            cost_estimate=cost(6 * rows * width * hid, 6 * width * hid + 6 * rows * width),
-            name="forward",
-        )(spot, ramp_step, *tok, gain, *on_chip(wg, wu, wd))
-        return (*outs[:5], [outs[5 + c * n3 : 5 + (c + 1) * n3] for c in range(CORES)])
+            compiler_params=limit(6),
+            cost_estimate=cost(2 * rows * width * hid, 2 * width * hid + 2 * rows * width),
+            name="out",
+        )(*on_chip(outs[3], wd))
+        return (*outs, [parts[c * n3 : (c + 1) * n3] for c in range(CORES)])
     outs = pl.pallas_call(
         functools.partial(forward_kernel, pieces=pieces, steps=steps, width=width, top=top),
         grid=(2 * steps,),
@@ -629,7 +665,7 @@
                 pltpu.VMEM((width // META + 8, META), jnp.float32),
                 pltpu.SemaphoreType.DMA((width // WIDE * (1 + CORES * n3),)),
             ],
-            compiler_params=pltpu.CompilerParams(vmem_limit_bytes=VMEM_MIB * 2**20),
+            compiler_params=limit(12),
             cost_estimate=cost(6 * rows * width * hid, 6 * width * hid + 6 * rows * width),
             name="backward",
         )(spot, *grad, *tok, *on_chip(wd, wg, wu, pre_gate, pre_up, side))
@@ -724,22 +760,22 @@
     wg, wu, wd = w_gate[0], w_up[0], w_down[0]
     if tokens.shape[0] * seq_count * ep_count <= WHOLE_ROWS:
         held = []
-        for weight in (wg, wu, wd):
+        for weight in (wg, wu):
             held += prefetch(spot, [weight])
-        wg, wu, wd = held
+        wg, wu = held
     scaled, pre_gate, pre_up, hidden, side, out_parts = forward(
         torus, tok, gain, wg, wu, wd, spot, ramp_step, top
     )
     og_all, pre_grads, parts = backward(torus, spot, grad, tok, wd, wg, wu, pre_gate, pre_up, side)
     w_gate_grad, w_up_grad = up_grads(scaled, pre_grads)
-    mixed, w_gate_grad = scatter_sum(torus, out_parts, w_gate_grad)
+    w_down_grad = down_grad(hidden, og_all)
+    mixed, w_down_grad = scatter_sum(torus, out_parts, w_down_grad)
     mixed = mixed.astype(jnp.bfloat16)
     total = scatter_sum(torus, parts)
     normed_grad = total[:, :width]
     count = gain_rows(span)
     gain_part = total[:count, width:] + total[count : 2 * count, width:]
     gain_grad = lax.dynamic_slice(gain_part.reshape(-1), (start,), (span,))
-    w_down_grad = down_grad(hidden, og_all)[None]
     own = tokens.astype(jnp.float32)
     own_recip = lax.rsqrt(jnp.mean(own * own, axis=1, keepdims=True) + norm_eps)
     weighted = gain * normed_grad
@@ -747,7 +783,7 @@
     tokens_grad = (
         own_recip * weighted - own * own_recip * own_recip * own_recip * inner / width
     ).astype(jnp.bfloat16)
-    return (mixed, tokens_grad, gain_grad, w_gate_grad[None], w_up_grad[None], w_down_grad)
+    return (mixed, tokens_grad, gain_grad, w_gate_grad[None], w_up_grad[None], w_down_grad[None])
 
 
 def solution(mesh):

time: 153 us -> 147 us (0.961)
  Pallas kernels: 39.6 us -> 36.3 us
  starting transfers between devices: 43.2 us -> 41.4 us
    pallas_call x3 -> x2, Pallas kernels: 10.9 us -> 7.26 us  [prefetch(): pl.pallas_call(prefetch_kernel, in_specs=[pl.BlockSpec(memory_space=pltpu...]
    pallas_call x0 -> x3, Pallas kernels: none -> 3.33 us  [the longest x1 3.28 us: forward(): pl.pallas_call(out_whole, in_specs=[vmem] * 2, out_specs=[hbm] * (CORES *...]
    pallas_call x1, Pallas kernels: 8.22 us -> 5.16 us  [forward(): pl.pallas_call(functools.partial(forward_whole, pieces=pieces, width=widt...]
    ppermute x44, starting transfers between devices: 43.2 us -> 41.4 us  [shift_rows(): return lax.ppermute(rows, AXES, torus.pairs(step, shift))]
  transfers between devices with their start and end apart: 44 -> 44, of which waited for: 14 -> 12; matrix products, arithmetic and copies ran while one was open for 2% -> 2% of each run, Pallas kernels for 25% -> 25%
where the time goes in v1:
time: 147 us; the launch traced here: 146 us
  waiting for transfers between devices  62.8 us (43%)
  starting transfers between devices  41.4 us (28%)
  Pallas kernels  36.3 us (25%)
  other arithmetic  3.16 us (2%)
  local copies, waits for them, and re-layouts  1.7 us (1%)
    ppermute x44, waiting for transfers between devices, shift_rows(): return lax.ppermute(rows, AXES, torus.pairs(step, shift))  62.8 us
    ppermute x44, starting transfers between devices, shift_rows(): return lax.ppermute(rows, AXES, torus.pairs(step, shift))  41.4 us
    pallas_call x1, Pallas kernels, backward(): pl.pallas_call(functools.partial(backward_whole, pieces=pieces, width=wid...  8.43 us
    pallas_call x2, Pallas kernels, prefetch(): pl.pallas_call(prefetch_kernel, in_specs=[pl.BlockSpec(memory_space=pltpu...  7.26 us
    pallas_call x1, Pallas kernels, up_grads(): pl.pallas_call(up_grads_kernel, grid=(width // step,), in_specs=[pl.Block...  6.36 us
    pallas_call x1, Pallas kernels, forward(): pl.pallas_call(functools.partial(forward_whole, pieces=pieces, width=widt...  5.16 us
    pallas_call x1, Pallas kernels, down_grad(): pl.pallas_call(down_grad_kernel, grid=(width // step,), in_specs=[pl.Bloc...  4.71 us
    pallas_call x1, Pallas kernels, forward(): pl.pallas_call(out_whole, in_specs=[vmem] * 2, out_specs=[hbm] * (CORES *...  3.28 us
  transfers between devices with their start and end apart: 44, of which 12 were waited for; matrix products, arithmetic and copies ran while one was open for 2% of the time, Pallas kernels for 25%

profile of v1, /device:TPU:0, one launch (start us, length us, event | category | flops | bytes accessed | tf_op | source)
XLA Modules:
  0.0 146.3 jit_solution(12637574468684072036)
XLA Ops:
  0.6 3.1 %collective-permute-start.29 = (bf16[8,7168]{1,0:T(8,128)(2,1)}, bf16[8,7168]{1,0:T(8,128)(2,1)S(1)}, u32[]{:S(2)}, u32[]{:S(2)}) collective-permute-start(bf16[8,7168]{1,0:T(8,128)(2,1)} %param.10), channel_id=1, source_target_pairs={{0,2},{1,17},{2,0},{3,19},{4,6},{5,21},{6,4},{7,23},{8,10},{9,25},... | collective-permute-start | bytes 344072 | tf_op jit(solution)/shard_map/ppermute | solution.py:83
  3.7 3.6 %collective-permute-start.21 = (bf16[8,7168]{1,0:T(8,128)(2,1)}, bf16[8,7168]{1,0:T(8,128)(2,1)S(1)}, u32[]{:S(2)}, u32[]{:S(2)}) collective-permute-start(bf16[8,7168]{1,0:T(8,128)(2,1)} %param.10), channel_id=1, source_target_pairs={{0,12},{1,13},{2,14},{3,15},{4,8},{5,9},{6,10},{7,11},{8,4},{9,5},... | collective-permute-start | bytes 344072 | tf_op jit(solution)/shard_map/ppermute | solution.py:83
  10.6 3.6 %prefetch.2.refs_13_.refs_22_ = bf16[7168,512]{1,0:T(8,128)(2,1)S(1)} custom-call(u32[3]{0:T(128)S(1)} %pad_add_fusion._.refs_0_, bf16[7168,512]{1,0:T(8,128)(2,1)} %bitcast.17), custom_call_target="tpu_custom_call" | custom-call | tf_op jit(solution)/shard_map/prefetch/pallas_call | solution.py:382
  14.3 3.6 %prefetch.3.refs_14_.refs_23_ = bf16[7168,512]{1,0:T(8,128)(2,1)S(1)} custom-call(u32[3]{0:T(128)S(1)} %pad_add_fusion._.refs_0_, bf16[7168,512]{1,0:T(8,128)(2,1)} %bitcast.18), custom_call_target="tpu_custom_call" | custom-call | tf_op jit(solution)/shard_map/prefetch/pallas_call | solution.py:382
  19.4 3.6 %collective-permute-start.2 = (bf16[8,7296]{1,0:T(8,128)(2,1)S(1)}, bf16[8,7296]{1,0:T(8,128)(2,1)S(1)}, u32[]{:S(2)}, u32[]{:S(2)}) collective-permute-start(bf16[8,7296]{1,0:T(8,128)(2,1)S(1)} %pack.1), channel_id=1, source_target_pairs={{0,12},{1,13},{2,14},{3,15},{4,8},{5,9},{6,10},{7,11},{8,4},{9,5},... | collective-permute-start | bytes 350216 | tf_op jit(solution)/shard_map/ppermute | solution.py:83
  23.9 2.6 %collective-permute-done.2.refs_2_ = bf16[8,7296]{1,0:T(8,128)(2,1)S(1)} collective-permute-done((bf16[8,7296]{1,0:T(8,128)(2,1)S(1)}, bf16[8,7296]{1,0:T(8,128)(2,1)S(1)}, u32[]{:S(2)}, u32[]{:S(2)}) %collective-permute-start.2) | collective-permute-done | bytes 116768 | tf_op jit(solution)/shard_map/ppermute | solution.py:83
  27.6 3.6 %collective-permute-done.1.refs_1_ = bf16[8,7296]{1,0:T(8,128)(2,1)S(1)} collective-permute-done((bf16[8,7296]{1,0:T(8,128)(2,1)S(1)}, bf16[8,7296]{1,0:T(8,128)(2,1)S(1)}, u32[]{:S(2)}, u32[]{:S(2)}) %collective-permute-start.1) | collective-permute-done | bytes 116768 | tf_op jit(solution)/shard_map/ppermute | solution.py:83
  33.8 1.5 %collective-permute-start.12 = (bf16[8,7296]{1,0:T(8,128)(2,1)S(1)}, bf16[8,7296]{1,0:T(8,128)(2,1)S(1)}, u32[]{:S(2)}, u32[]{:S(2)}) collective-permute-start(bf16[8,7296]{1,0:T(8,128)(2,1)S(1)} %collective-permute-done.10), channel_id=1, source_target_pairs={{0,16},{1,3},{2,18},{3,1},{4,20},{5,7},{6,22},{7,5},{8,24},{9,11},... | collective-permute-start | bytes 350216 | tf_op jit(solution)/shard_map/ppermute | solution.py:83
  35.3 1.6 %collective-permute-start.22 = (bf16[24,7168]{1,0:T(8,128)(2,1)S(1)}, bf16[24,7168]{1,0:T(8,128)(2,1)S(1)}, u32[]{:S(2)}, u32[]{:S(2)}) collective-permute-start(bf16[24,7168]{1,0:T(8,128)(2,1)S(1)} %join.3.refs_1_), channel_id=1, source_target_pairs={{0,2},{1,17},{2,0},{3,19},{4,6},{5,21},{6,4},{7,23},{8,10},{9,25},... | collective-permute-start | bytes 1032200 | tf_op jit(solution)/shard_map/ppermute | solution.py:83
  36.9 7.6 %collective-permute-done.31 = bf16[8,7168]{1,0:T(8,128)(2,1)S(1)} collective-permute-done((bf16[8,7168]{1,0:T(8,128)(2,1)S(1)}, bf16[8,7168]{1,0:T(8,128)(2,1)S(1)}, u32[]{:S(2)}, u32[]{:S(2)}) %collective-permute-start.31) | collective-permute-done | bytes 114720 | tf_op jit(solution)/shard_map/ppermute | solution.py:83
  44.6 2.5 %collective-permute-done.12 = bf16[8,7296]{1,0:T(8,128)(2,1)S(1)} collective-permute-done((bf16[8,7296]{1,0:T(8,128)(2,1)S(1)}, bf16[8,7296]{1,0:T(8,128)(2,1)S(1)}, u32[]{:S(2)}, u32[]{:S(2)}) %collective-permute-start.12) | collective-permute-done | bytes 116768 | tf_op jit(solution)/shard_map/ppermute | solution.py:83
  47.1 1.5 %collective-permute-start.4 = (bf16[24,7296]{1,0:T(8,128)(2,1)S(1)}, bf16[24,7296]{1,0:T(8,128)(2,1)S(1)}, u32[]{:S(2)}, u32[]{:S(2)}) collective-permute-start(bf16[24,7296]{1,0:T(8,128)(2,1)S(1)} %join.2.refs_2_.refs_11_), channel_id=1, source_target_pairs={{0,16},{1,3},{2,18},{3,1},{4,20},{5,7},{6,22},{7,5},{8,24},{9,11},... | collective-permute-start | bytes 1050632 | tf_op jit(solution)/shard_map/ppermute | solution.py:83
  49.2 1.6 %collective-permute-start.24 = (bf16[24,7168]{1,0:T(8,128)(2,1)S(1)}, bf16[24,7168]{1,0:T(8,128)(2,1)S(1)}, u32[]{:S(2)}, u32[]{:S(2)}) collective-permute-start(bf16[24,7168]{1,0:T(8,128)(2,1)S(1)} %collective-permute-done.22.refs_2_), channel_id=1, source_target_pairs={{0,16},{1,3},{2,18},{3,1},{4,20},{5,7},{6,22},{7,5},{8,24},{9,11},... | collective-permute-start | bytes 1032200 | tf_op jit(solution)/shard_map/ppermute | solution.py:83
  50.8 3.6 %collective-permute-done.4.refs_4_.refs_13_ = bf16[24,7296]{1,0:T(8,128)(2,1)S(1)} collective-permute-done((bf16[24,7296]{1,0:T(8,128)(2,1)S(1)}, bf16[24,7296]{1,0:T(8,128)(2,1)S(1)}, u32[]{:S(2)}, u32[]{:S(2)}) %collective-permute-start.4) | collective-permute-done | bytes 350240 | tf_op jit(solution)/shard_map/ppermute | solution.py:83
  54.4 3.7 %collective-permute-done.5.refs_5_.refs_14_ = bf16[24,7296]{1,0:T(8,128)(2,1)S(1)} collective-permute-done((bf16[24,7296]{1,0:T(8,128)(2,1)S(1)}, bf16[24,7296]{1,0:T(8,128)(2,1)S(1)}, u32[]{:S(2)}, u32[]{:S(2)}) %collective-permute-start.5) | collective-permute-done | bytes 350240 | tf_op jit(solution)/shard_map/ppermute | solution.py:83
  58.7 3.1 %collective-permute-done.24.refs_4_ = bf16[24,7168]{1,0:T(8,128)(2,1)S(1)} collective-permute-done((bf16[24,7168]{1,0:T(8,128)(2,1)S(1)}, bf16[24,7168]{1,0:T(8,128)(2,1)S(1)}, u32[]{:S(2)}, u32[]{:S(2)}) %collective-permute-start.24) | collective-permute-done | bytes 344096 | tf_op jit(solution)/shard_map/ppermute | solution.py:83
  62.9 5.2 %forward.1 = (bf16[256,7168]{1,0:T(8,128)(2,1)S(1)}, f32[256,512]{1,0:T(8,128)S(1)}, f32[256,512]{1,0:T(8,128)S(1)}, bf16[256,512]{1,0:T(8,128)(2,1)S(1)}, f32[256,128]{1,0:T(8,128)S(1)}) custom-call(u32[3]{0:T(128)S(1)} %pad_add_fusion._.refs_0_, s32[16]{0:T(128)S(1)} %copy-done.1, bf16[24,7296]{1,0:T(8,128)(2,1)S(1)} %join.2.refs_2_.refs_11_, ...), custom_call_target="tpu_custom_call" | custom-call | flops 3758096384 | bytes 22020096 | tf_op jit(solution)/shard_map/forward/pallas_call | solution.py:577
  68.1 3.3 %out.1 = (bf16[64,7168]{1,0:T(8,128)(2,1)}, bf16[64,7168]{1,0:T(8,128)(2,1)}, bf16[64,7168]{1,0:T(8,128)(2,1)}, bf16[64,7168]{1,0:T(8,128)(2,1)}) custom-call(bf16[256,512]{1,0:T(8,128)(2,1)S(1)} %get-tuple-element.25.hidden, bf16[512,7168]{1,0:T(8,128)(2,1)S(1)} %bitcast.14), custom_call_target="tpu_custom_call" | custom-call | flops 1879048192 | bytes 11010048 | tf_op jit(solution)/shard_map/out/pallas_call | solution.py:587
  71.5 8.4 %backward.1 = (bf16[256,7168]{1,0:T(8,128)(2,1)S(1)}, bf16[256,1024]{1,0:T(8,128)(2,1)S(1)}, bf16[64,7296]{1,0:T(8,128)(2,1)}, bf16[64,7296]{1,0:T(8,128)(2,1)},...) custom-call(u32[3]{0:T(128)S(1)} %pad_add_fusion._.refs_0_, bf16[24,7168]{1,0:T(8,128)(2,1)S(1)} %join.3.refs_1_, ...), custom_call_target="tpu_custom_call" | custom-call | flops 5637144576 | bytes 33030144 | tf_op jit(solution)/shard_map/backward/pallas_call | solution.py:655
  81.0 4.7 %down_grad.1 = bf16[512,7168]{1,0:T(8,128)(2,1)} custom-call(bf16[256,512]{1,0:T(8,128)(2,1)S(1)} %get-tuple-element.25.hidden, bf16[256,7168]{1,0:T(8,128)(2,1)S(1)} %get-tuple-element.33.og_all), custom_call_target="tpu_custom_call" | custom-call | flops 1879048192 | bytes 11010048 | tf_op jit(solution)/shard_map/down_grad/pallas_call | solution.py:730
  85.7 6.4 %up_grads.1 = (bf16[7168,512]{1,0:T(8,128)(2,1)}, bf16[7168,512]{1,0:T(8,128)(2,1)}) custom-call(bf16[256,7168]{1,0:T(8,128)(2,1)S(1)} %get-tuple-element.39.scaled, bf16[256,1024]{1,0:T(8,128)(2,1)S(1)} %get-tuple-element.40.pre_grads), custom_call_target="tpu_custom_call" | custom-call | flops 3758096384 | bytes 18350080 | tf_op jit(solution)/shard_map/up_grads/pallas_call | solution.py:711
  92.3 1.6 %collective-permute-start.16 = (bf16[32,7168]{1,0:T(8,128)(2,1)S(1)}, bf16[32,7168]{1,0:T(8,128)(2,1)S(1)}, u32[]{:S(2)}, u32[]{:S(2)}) collective-permute-start(bf16[32,7168]{1,0:T(8,128)(2,1)S(1)} %get-tuple-element.52), channel_id=1, source_target_pairs={{0,16},{1,3},{2,18},{3,1},{4,20},{5,7},{6,22},{7,5},{8,24},{9,11},... | collective-permute-start | bytes 1376264 | tf_op jit(solution)/shard_map/ppermute | solution.py:83
  94.6 1.6 %collective-permute-start.38 = (bf16[32,7296]{1,0:T(8,128)(2,1)S(1)}, bf16[32,7296]{1,0:T(8,128)(2,1)S(1)}, u32[]{:S(2)}, u32[]{:S(2)}) collective-permute-start(bf16[32,7296]{1,0:T(8,128)(2,1)S(1)} %get-tuple-element.50), channel_id=1, source_target_pairs={{0,16},{1,3},{2,18},{3,1},{4,20},{5,7},{6,22},{7,5},{8,24},{9,11},... | collective-permute-start | bytes 1400840 | tf_op jit(solution)/shard_map/ppermute | solution.py:83
  96.7 9.0 %collective-permute-done.17 = bf16[32,7168]{1,0:T(8,128)(2,1)S(1)} collective-permute-done((bf16[32,7168]{1,0:T(8,128)(2,1)S(1)}, bf16[32,7168]{1,0:T(8,128)(2,1)S(1)}, u32[]{:S(2)}, u32[]{:S(2)}) %collective-permute-start.17) | collective-permute-done | bytes 458784 | tf_op jit(solution)/shard_map/ppermute | solution.py:83
  106.6 14.1 %collective-permute-done.39 = bf16[32,7296]{1,0:T(8,128)(2,1)S(1)} collective-permute-done((bf16[32,7296]{1,0:T(8,128)(2,1)S(1)}, bf16[32,7296]{1,0:T(8,128)(2,1)S(1)}, u32[]{:S(2)}, u32[]{:S(2)}) %collective-permute-start.39) | collective-permute-done | bytes 466976 | tf_op jit(solution)/shard_map/ppermute | solution.py:83
  121.8 2.2 %collective-permute-start.33 = (bf16[8,7168]{1,0:T(8,128)(2,1)S(1)}, bf16[8,7168]{1,0:T(8,128)(2,1)S(1)}, u32[]{:S(2)}, u32[]{:S(2)}) collective-permute-start(bf16[8,7168]{1,0:T(8,128)(2,1)S(1)} %get-tuple-element.57), channel_id=1, source_target_pairs={{0,12},{1,13},{2,14},{3,15},{4,8},{5,9},{6,10},{7,11},{8,4},{9,5},... | collective-permute-start | bytes 344072 | tf_op jit(solution)/shard_map/ppermute | solution.py:83
  124.0 2.2 %collective-permute-start.34 = (bf16[8,7168]{1,0:T(8,128)(2,1)S(1)}, bf16[8,7168]{1,0:T(8,128)(2,1)S(1)}, u32[]{:S(2)}, u32[]{:S(2)}) collective-permute-start(bf16[8,7168]{1,0:T(8,128)(2,1)S(1)} %get-tuple-element.59), channel_id=1, source_target_pairs={{0,8},{1,9},{2,10},{3,11},{4,12},{5,13},{6,14},{7,15},{8,0},{9,1},... | collective-permute-start | bytes 344072 | tf_op jit(solution)/shard_map/ppermute | solution.py:83
  126.2 3.3 %collective-permute-done.40 = bf16[32,7296]{1,0:T(8,128)(2,1)S(1)} collective-permute-done((bf16[32,7296]{1,0:T(8,128)(2,1)S(1)}, bf16[32,7296]{1,0:T(8,128)(2,1)S(1)}, u32[]{:S(2)}, u32[]{:S(2)}) %collective-permute-start.40) | collective-permute-done | bytes 466976 | tf_op jit(solution)/shard_map/ppermute | solution.py:83
  129.8 2.3 %collective-permute-start.41 = (bf16[8,7296]{1,0:T(8,128)(2,1)S(1)}, bf16[8,7296]{1,0:T(8,128)(2,1)S(1)}, u32[]{:S(2)}, u32[]{:S(2)}) collective-permute-start(bf16[8,7296]{1,0:T(8,128)(2,1)S(1)} %get-tuple-element.54), channel_id=1, source_target_pairs={{0,12},{1,13},{2,14},{3,15},{4,8},{5,9},{6,10},{7,11},{8,4},{9,5},... | collective-permute-start | bytes 350216 | tf_op jit(solution)/shard_map/ppermute | solution.py:83
  132.2 2.0 %collective-permute-start.42 = (bf16[8,7296]{1,0:T(8,128)(2,1)S(1)}, bf16[8,7296]{1,0:T(8,128)(2,1)S(1)}, u32[]{:S(2)}, u32[]{:S(2)}) collective-permute-start(bf16[8,7296]{1,0:T(8,128)(2,1)S(1)} %get-tuple-element.56), channel_id=1, source_target_pairs={{0,8},{1,9},{2,10},{3,11},{4,12},{5,13},{6,14},{7,15},{8,0},{9,1},... | collective-permute-start | bytes 350216 | tf_op jit(solution)/shard_map/ppermute | solution.py:83
  134.2 5.0 %collective-permute-done.34 = bf16[8,7168]{1,0:T(8,128)(2,1)S(1)} collective-permute-done((bf16[8,7168]{1,0:T(8,128)(2,1)S(1)}, bf16[8,7168]{1,0:T(8,128)(2,1)S(1)}, u32[]{:S(2)}, u32[]{:S(2)}) %collective-permute-start.34) | collective-permute-done | bytes 114720 | tf_op jit(solution)/shard_map/ppermute | solution.py:83
  139.9 4.6 %collective-permute-done.42 = bf16[8,7296]{1,0:T(8,128)(2,1)S(1)} collective-permute-done((bf16[8,7296]{1,0:T(8,128)(2,1)S(1)}, bf16[8,7296]{1,0:T(8,128)(2,1)S(1)}, u32[]{:S(2)}, u32[]{:S(2)}) %collective-permute-start.42) | collective-permute-done | bytes 116768 | tf_op jit(solution)/shard_map/ppermute | solution.py:83
  (108 shorter events, 19.1 us)
Async XLA Ops:
  0.6 18.3 %collective-permute-start.29 = (bf16[8,7168]{1,0:T(8,128)(2,1)}, bf16[8,7168]{1,0:T(8,128)(2,1)S(1)}, u32[]{:S(2)}, u32[]{:S(2)}) collective-permute-start(bf16[8,7168]{1,0:T(8,128)(2,1)} %param.10), channel_id=1, source_target_pairs={{0,2},{1,17},{2,0},{3,19},{4,6},{5,21},{6,4},{7,23},{8,10},{9,25},... | collective-permute-start | bytes 344072 | tf_op jit(solution)/shard_map/ppermute | solution.py:83
  3.7 15.7 %collective-permute-start.21 = (bf16[8,7168]{1,0:T(8,128)(2,1)}, bf16[8,7168]{1,0:T(8,128)(2,1)S(1)}, u32[]{:S(2)}, u32[]{:S(2)}) collective-permute-start(bf16[8,7168]{1,0:T(8,128)(2,1)} %param.10), channel_id=1, source_target_pairs={{0,12},{1,13},{2,14},{3,15},{4,8},{5,9},{6,10},{7,11},{8,4},{9,5},... | collective-permute-start | bytes 344072 | tf_op jit(solution)/shard_map/ppermute | solution.py:83
  7.3 15.7 %collective-permute-start.20 = (bf16[8,7168]{1,0:T(8,128)(2,1)}, bf16[8,7168]{1,0:T(8,128)(2,1)S(1)}, u32[]{:S(2)}, u32[]{:S(2)}) collective-permute-start(bf16[8,7168]{1,0:T(8,128)(2,1)} %param.10), channel_id=1, source_target_pairs={{0,8},{1,9},{2,10},{3,11},{4,12},{5,13},{6,14},{7,15},{8,0},{9,1},... | collective-permute-start | bytes 344072 | tf_op jit(solution)/shard_map/ppermute | solution.py:83
  7.3 15.7 %collective-permute-start.19 = (bf16[8,7168]{1,0:T(8,128)(2,1)}, bf16[8,7168]{1,0:T(8,128)(2,1)S(1)}, u32[]{:S(2)}, u32[]{:S(2)}) collective-permute-start(bf16[8,7168]{1,0:T(8,128)(2,1)} %param.10), channel_id=1, source_target_pairs={{0,4},{1,5},{2,6},{3,7},{4,0},{5,1},{6,2},{7,3},{8,12},{9,13},{10,... | collective-permute-start | bytes 344072 | tf_op jit(solution)/shard_map/ppermute | solution.py:83
  8.1 25.2 %collective-permute-start.30 = (bf16[8,7168]{1,0:T(8,128)(2,1)}, bf16[8,7168]{1,0:T(8,128)(2,1)S(1)}, u32[]{:S(2)}, u32[]{:S(2)}) collective-permute-start(bf16[8,7168]{1,0:T(8,128)(2,1)} %param.10), channel_id=1, source_target_pairs={{0,16},{1,3},{2,18},{3,1},{4,20},{5,7},{6,22},{7,5},{8,24},{9,11},... | collective-permute-start | bytes 344072 | tf_op jit(solution)/shard_map/ppermute | solution.py:83
  18.9 14.9 %collective-permute-start.10 = (bf16[8,7296]{1,0:T(8,128)(2,1)S(1)}, bf16[8,7296]{1,0:T(8,128)(2,1)S(1)}, u32[]{:S(2)}, u32[]{:S(2)}) collective-permute-start(bf16[8,7296]{1,0:T(8,128)(2,1)S(1)} %pack.1), channel_id=1, source_target_pairs={{0,2},{1,17},{2,0},{3,19},{4,6},{5,21},{6,4},{7,23},{8,10},{9,25},... | collective-permute-start | bytes 350216 | tf_op jit(solution)/shard_map/ppermute | solution.py:83
  23.0 9.6 %collective-permute-start = (bf16[8,7296]{1,0:T(8,128)(2,1)S(1)}, bf16[8,7296]{1,0:T(8,128)(2,1)S(1)}, u32[]{:S(2)}, u32[]{:S(2)}) collective-permute-start(bf16[8,7296]{1,0:T(8,128)(2,1)S(1)} %pack.1), channel_id=1, source_target_pairs={{0,4},{1,5},{2,6},{3,7},{4,0},{5,1},{6,2},{7,3},{8,12},{9,13},{10,... | collective-permute-start | bytes 350216 | tf_op jit(solution)/shard_map/ppermute | solution.py:83
  31.2 18.0 %collective-permute-start.23 = (bf16[24,7168]{1,0:T(8,128)(2,1)S(1)}, bf16[24,7168]{1,0:T(8,128)(2,1)S(1)}, u32[]{:S(2)}, u32[]{:S(2)}) collective-permute-start(bf16[24,7168]{1,0:T(8,128)(2,1)S(1)} %join.3.refs_1_), channel_id=1, source_target_pairs={{0,16},{1,3},{2,18},{3,1},{4,20},{5,7},{6,22},{7,5},{8,24},{9,11},... | collective-permute-start | bytes 1032200 | tf_op jit(solution)/shard_map/ppermute | solution.py:83
  32.7 11.9 %collective-permute-start.31 = (bf16[8,7168]{1,0:T(8,128)(2,1)S(1)}, bf16[8,7168]{1,0:T(8,128)(2,1)S(1)}, u32[]{:S(2)}, u32[]{:S(2)}) collective-permute-start(bf16[8,7168]{1,0:T(8,128)(2,1)S(1)} %collective-permute-done.29), channel_id=1, source_target_pairs={{0,16},{1,3},{2,18},{3,1},{4,20},{5,7},{6,22},{7,5},{8,24},{9,11},... | collective-permute-start | bytes 344072 | tf_op jit(solution)/shard_map/ppermute | solution.py:83
  33.2 15.3 %collective-permute-start.3 = (bf16[24,7296]{1,0:T(8,128)(2,1)S(1)}, bf16[24,7296]{1,0:T(8,128)(2,1)S(1)}, u32[]{:S(2)}, u32[]{:S(2)}) collective-permute-start(bf16[24,7296]{1,0:T(8,128)(2,1)S(1)} %join.2.refs_2_.refs_11_), channel_id=1, source_target_pairs={{0,2},{1,17},{2,0},{3,19},{4,6},{5,21},{6,4},{7,23},{8,10},{9,25},... | collective-permute-start | bytes 1050632 | tf_op jit(solution)/shard_map/ppermute | solution.py:83
  33.8 13.2 %collective-permute-start.12 = (bf16[8,7296]{1,0:T(8,128)(2,1)S(1)}, bf16[8,7296]{1,0:T(8,128)(2,1)S(1)}, u32[]{:S(2)}, u32[]{:S(2)}) collective-permute-start(bf16[8,7296]{1,0:T(8,128)(2,1)S(1)} %collective-permute-done.10), channel_id=1, source_target_pairs={{0,16},{1,3},{2,18},{3,1},{4,20},{5,7},{6,22},{7,5},{8,24},{9,11},... | collective-permute-start | bytes 350216 | tf_op jit(solution)/shard_map/ppermute | solution.py:83
  35.3 13.9 %collective-permute-start.22 = (bf16[24,7168]{1,0:T(8,128)(2,1)S(1)}, bf16[24,7168]{1,0:T(8,128)(2,1)S(1)}, u32[]{:S(2)}, u32[]{:S(2)}) collective-permute-start(bf16[24,7168]{1,0:T(8,128)(2,1)S(1)} %join.3.refs_1_), channel_id=1, source_target_pairs={{0,2},{1,17},{2,0},{3,19},{4,6},{5,21},{6,4},{7,23},{8,10},{9,25},... | collective-permute-start | bytes 1032200 | tf_op jit(solution)/shard_map/ppermute | solution.py:83
  48.6 9.6 %collective-permute-start.5 = (bf16[24,7296]{1,0:T(8,128)(2,1)S(1)}, bf16[24,7296]{1,0:T(8,128)(2,1)S(1)}, u32[]{:S(2)}, u32[]{:S(2)}) collective-permute-start(bf16[24,7296]{1,0:T(8,128)(2,1)S(1)} %collective-permute-done.3.refs_3_.refs_12_), channel_id=1, source_target_pairs={{0,16},{1,3},{2,18},{3,1},{4,20},{5,7},{6,22},{7,5},{8,24},{9,11},... | collective-permute-start | bytes 1050632 | tf_op jit(solution)/shard_map/ppermute | solution.py:83
  49.2 12.6 %collective-permute-start.24 = (bf16[24,7168]{1,0:T(8,128)(2,1)S(1)}, bf16[24,7168]{1,0:T(8,128)(2,1)S(1)}, u32[]{:S(2)}, u32[]{:S(2)}) collective-permute-start(bf16[24,7168]{1,0:T(8,128)(2,1)S(1)} %collective-permute-done.22.refs_2_), channel_id=1, source_target_pairs={{0,16},{1,3},{2,18},{3,1},{4,20},{5,7},{6,22},{7,5},{8,24},{9,11},... | collective-permute-start | bytes 1032200 | tf_op jit(solution)/shard_map/ppermute | solution.py:83
  50.8 11.5 %collective-permute-start.7 = (bf16[24,7296]{1,0:T(8,128)(2,1)S(1)}, bf16[24,7296]{1,0:T(8,128)(2,1)S(1)}, u32[]{:S(2)}, u32[]{:S(2)}) collective-permute-start(bf16[24,7296]{1,0:T(8,128)(2,1)S(1)} %collective-permute-done.3.refs_3_.refs_12_), channel_id=1, source_target_pairs={{0,1},{1,0},{2,3},{3,2},{4,5},{5,4},{6,7},{7,6},{8,9},{9,8},{10,11... | collective-permute-start | bytes 1050632 | tf_op jit(solution)/shard_map/ppermute | solution.py:83
  58.2 13.2 %collective-permute-start.25 = (bf16[24,7168]{1,0:T(8,128)(2,1)S(1)}, bf16[24,7168]{1,0:T(8,128)(2,1)S(1)}, u32[]{:S(2)}, u32[]{:S(2)}) collective-permute-start(bf16[24,7168]{1,0:T(8,128)(2,1)S(1)} %join.3.refs_1_), channel_id=1, source_target_pairs={{0,1},{1,0},{2,3},{3,2},{4,5},{5,4},{6,7},{7,6},{8,9},{9,8},{10,11... | collective-permute-start | bytes 1032200 | tf_op jit(solution)/shard_map/ppermute | solution.py:83
  61.8 9.7 %collective-permute-start.32 = (bf16[32,7168]{1,0:T(8,128)(2,1)S(1)}, bf16[32,7168]{1,0:T(8,128)(2,1)S(1)}, u32[]{:S(2)}, u32[]{:S(2)}) collective-permute-start(bf16[32,7168]{1,0:T(8,128)(2,1)S(1)} %constant_dynamic-update-slice_fusion.refs_9_), channel_id=1, source_target_pairs={{0,1},{1,0},{2,3},{3,2},{4,5},{5,4},{6,7},{7,6},{8,9},{9,8},{10,11... | collective-permute-start | bytes 1376264 | tf_op jit(solution)/shard_map/ppermute | solution.py:83
  61.8 9.7 %collective-permute-start.26 = (bf16[24,7168]{1,0:T(8,128)(2,1)S(1)}, bf16[24,7168]{1,0:T(8,128)(2,1)S(1)}, u32[]{:S(2)}, u32[]{:S(2)}) collective-permute-start(bf16[24,7168]{1,0:T(8,128)(2,1)S(1)} %collective-permute-done.22.refs_2_), channel_id=1, source_target_pairs={{0,1},{1,0},{2,3},{3,2},{4,5},{5,4},{6,7},{7,6},{8,9},{9,8},{10,11... | collective-permute-start | bytes 1032200 | tf_op jit(solution)/shard_map/ppermute | solution.py:83
  71.4 20.7 %collective-permute-start.15 = (bf16[64,7168]{1,0:T(8,128)(2,1)}, bf16[64,7168]{1,0:T(8,128)(2,1)S(1)}, u32[]{:S(2)}, u32[]{:S(2)}) collective-permute-start(bf16[64,7168]{1,0:T(8,128)(2,1)} %get-tuple-element.29), channel_id=1, source_target_pairs={{0,1},{1,0},{2,3},{3,2},{4,5},{5,4},{6,7},{7,6},{8,9},{9,8},{10,11... | collective-permute-start | bytes 2752520 | tf_op jit(solution)/shard_map/ppermute | solution.py:83
  80.0 26.6 %collective-permute-start.36 = (bf16[64,7296]{1,0:T(8,128)(2,1)}, bf16[64,7296]{1,0:T(8,128)(2,1)S(1)}, u32[]{:S(2)}, u32[]{:S(2)}) collective-permute-start(bf16[64,7296]{1,0:T(8,128)(2,1)} %get-tuple-element.36), channel_id=1, source_target_pairs={{0,1},{1,0},{2,3},{3,2},{4,5},{5,4},{6,7},{7,6},{8,9},{9,8},{10,11... | collective-permute-start | bytes 2801672 | tf_op jit(solution)/shard_map/ppermute | solution.py:83
  80.5 13.9 %collective-permute-start.37 = (bf16[64,7296]{1,0:T(8,128)(2,1)}, bf16[64,7296]{1,0:T(8,128)(2,1)S(1)}, u32[]{:S(2)}, u32[]{:S(2)}) collective-permute-start(bf16[64,7296]{1,0:T(8,128)(2,1)} %get-tuple-element.38), channel_id=1, source_target_pairs={{0,1},{1,0},{2,3},{3,2},{4,5},{5,4},{6,7},{7,6},{8,9},{9,8},{10,11... | collective-permute-start | bytes 2801672 | tf_op jit(solution)/shard_map/ppermute | solution.py:83
  80.6 15.6 %collective-permute-start.14 = (bf16[64,7168]{1,0:T(8,128)(2,1)S(1)}, bf16[64,7168]{1,0:T(8,128)(2,1)S(1)}, u32[]{:S(2)}, u32[]{:S(2)}) collective-permute-start(bf16[64,7168]{1,0:T(8,128)(2,1)S(1)} %copy-done.7), channel_id=1, source_target_pairs={{0,1},{1,0},{2,3},{3,2},{4,5},{5,4},{6,7},{7,6},{8,9},{9,8},{10,11... | collective-permute-start | bytes 2752520 | tf_op jit(solution)/shard_map/ppermute | solution.py:83
  92.3 29.2 %collective-permute-start.16 = (bf16[32,7168]{1,0:T(8,128)(2,1)S(1)}, bf16[32,7168]{1,0:T(8,128)(2,1)S(1)}, u32[]{:S(2)}, u32[]{:S(2)}) collective-permute-start(bf16[32,7168]{1,0:T(8,128)(2,1)S(1)} %get-tuple-element.52), channel_id=1, source_target_pairs={{0,16},{1,3},{2,18},{3,1},{4,20},{5,7},{6,22},{7,5},{8,24},{9,11},... | collective-permute-start | bytes 1376264 | tf_op jit(solution)/shard_map/ppermute | solution.py:83
  93.8 11.9 %collective-permute-start.17 = (bf16[32,7168]{1,0:T(8,128)(2,1)S(1)}, bf16[32,7168]{1,0:T(8,128)(2,1)S(1)}, u32[]{:S(2)}, u32[]{:S(2)}) collective-permute-start(bf16[32,7168]{1,0:T(8,128)(2,1)S(1)} %get-tuple-element.53), channel_id=1, source_target_pairs={{0,16},{1,3},{2,18},{3,1},{4,20},{5,7},{6,22},{7,5},{8,24},{9,11},... | collective-permute-start | bytes 1376264 | tf_op jit(solution)/shard_map/ppermute | solution.py:83
  94.6 31.6 %collective-permute-start.38 = (bf16[32,7296]{1,0:T(8,128)(2,1)S(1)}, bf16[32,7296]{1,0:T(8,128)(2,1)S(1)}, u32[]{:S(2)}, u32[]{:S(2)}) collective-permute-start(bf16[32,7296]{1,0:T(8,128)(2,1)S(1)} %get-tuple-element.50), channel_id=1, source_target_pairs={{0,16},{1,3},{2,18},{3,1},{4,20},{5,7},{6,22},{7,5},{8,24},{9,11},... | collective-permute-start | bytes 1400840 | tf_op jit(solution)/shard_map/ppermute | solution.py:83
  96.2 24.5 %collective-permute-start.39 = (bf16[32,7296]{1,0:T(8,128)(2,1)S(1)}, bf16[32,7296]{1,0:T(8,128)(2,1)S(1)}, u32[]{:S(2)}, u32[]{:S(2)}) collective-permute-start(bf16[32,7296]{1,0:T(8,128)(2,1)S(1)} %get-tuple-element.51), channel_id=1, source_target_pairs={{0,16},{1,3},{2,18},{3,1},{4,20},{5,7},{6,22},{7,5},{8,24},{9,11},... | collective-permute-start | bytes 1400840 | tf_op jit(solution)/shard_map/ppermute | solution.py:83
  105.9 15.6 %collective-permute-start.18 = (bf16[32,7168]{1,0:T(8,128)(2,1)S(1)}, bf16[32,7168]{1,0:T(8,128)(2,1)S(1)}, u32[]{:S(2)}, u32[]{:S(2)}) collective-permute-start(bf16[32,7168]{1,0:T(8,128)(2,1)S(1)} %add_convert_fusion.3), channel_id=1, source_target_pairs={{0,2},{1,17},{2,0},{3,19},{4,6},{5,21},{6,4},{7,23},{8,10},{9,25},... | collective-permute-start | bytes 1376264 | tf_op jit(solution)/shard_map/ppermute | solution.py:83
  121.8 10.5 %collective-permute-start.33 = (bf16[8,7168]{1,0:T(8,128)(2,1)S(1)}, bf16[8,7168]{1,0:T(8,128)(2,1)S(1)}, u32[]{:S(2)}, u32[]{:S(2)}) collective-permute-start(bf16[8,7168]{1,0:T(8,128)(2,1)S(1)} %get-tuple-element.57), channel_id=1, source_target_pairs={{0,12},{1,13},{2,14},{3,15},{4,8},{5,9},{6,10},{7,11},{8,4},{9,5},... | collective-permute-start | bytes 344072 | tf_op jit(solution)/shard_map/ppermute | solution.py:83
  124.0 10.3 %collective-permute-start.35 = (bf16[8,7168]{1,0:T(8,128)(2,1)S(1)}, bf16[8,7168]{1,0:T(8,128)(2,1)S(1)}, u32[]{:S(2)}, u32[]{:S(2)}) collective-permute-start(bf16[8,7168]{1,0:T(8,128)(2,1)S(1)} %get-tuple-element.58), channel_id=1, source_target_pairs={{0,4},{1,5},{2,6},{3,7},{4,0},{5,1},{6,2},{7,3},{8,12},{9,13},{10,... | collective-permute-start | bytes 344072 | tf_op jit(solution)/shard_map/ppermute | solution.py:83
  124.0 15.2 %collective-permute-start.34 = (bf16[8,7168]{1,0:T(8,128)(2,1)S(1)}, bf16[8,7168]{1,0:T(8,128)(2,1)S(1)}, u32[]{:S(2)}, u32[]{:S(2)}) collective-permute-start(bf16[8,7168]{1,0:T(8,128)(2,1)S(1)} %get-tuple-element.59), channel_id=1, source_target_pairs={{0,8},{1,9},{2,10},{3,11},{4,12},{5,13},{6,14},{7,15},{8,0},{9,1},... | collective-permute-start | bytes 344072 | tf_op jit(solution)/shard_map/ppermute | solution.py:83
  129.8 10.2 %collective-permute-start.41 = (bf16[8,7296]{1,0:T(8,128)(2,1)S(1)}, bf16[8,7296]{1,0:T(8,128)(2,1)S(1)}, u32[]{:S(2)}, u32[]{:S(2)}) collective-permute-start(bf16[8,7296]{1,0:T(8,128)(2,1)S(1)} %get-tuple-element.54), channel_id=1, source_target_pairs={{0,12},{1,13},{2,14},{3,15},{4,8},{5,9},{6,10},{7,11},{8,4},{9,5},... | collective-permute-start | bytes 350216 | tf_op jit(solution)/shard_map/ppermute | solution.py:83
  132.2 12.3 %collective-permute-start.42 = (bf16[8,7296]{1,0:T(8,128)(2,1)S(1)}, bf16[8,7296]{1,0:T(8,128)(2,1)S(1)}, u32[]{:S(2)}, u32[]{:S(2)}) collective-permute-start(bf16[8,7296]{1,0:T(8,128)(2,1)S(1)} %get-tuple-element.56), channel_id=1, source_target_pairs={{0,8},{1,9},{2,10},{3,11},{4,12},{5,13},{6,14},{7,15},{8,0},{9,1},... | collective-permute-start | bytes 350216 | tf_op jit(solution)/shard_map/ppermute | solution.py:83
  (22 other events, 343.8 us)

commit v2 on v1

--- a/solution.py
+++ b/solution.py
@@ -239,17 +239,10 @@
     )(*off_chip(tokens, routes, gates))
 
 
-def send_parts(rows, parts, cols, sems, first):
+def store_parts(parts, cols, rows):
     size = parts[0].shape[0]
-    copies = [
-        pltpu.make_async_copy(
-            rows.at[p * size : (p + 1) * size, cols], ref.at[:, cols], sems.at[first + p]
-        )
-        for p, ref in enumerate(parts)
-    ]
-    for copy in copies:
-        copy.start()
-    return copies
+    for p, ref in enumerate(parts):
+        ref[:, cols] = rows[p * size : (p + 1) * size]
 
 
 def forward_whole(*refs, pieces, width, top):
@@ -257,7 +250,8 @@
     tok = refs[2 : 2 + pieces]
     gain, wg, wu = refs[2 + pieces : 5 + pieces]
     outs = refs[5 + pieces :]
-    scaled, pre_gate, pre_up, hidden, side, acc_g, acc_u = outs
+    scaled_out, pre_gate, pre_up, hidden, side, acc_g, acc_u, scaled, sems = outs
+    pending = []
     squares = []
     for k in range(width // WIDE):
         cols = slice(k * WIDE, (k + 1) * WIDE)
@@ -270,6 +264,8 @@
                 squares.append(part)
             else:
                 squares[p] = squares[p] + part
+        pending.append(pltpu.make_async_copy(scaled.at[:, cols], scaled_out.at[:, cols], sems.at[k]))
+        pending[-1].start()
         xs = scaled[:, cols]
         if k == 0:
             acc_g[...] = matmul(xs, wg[cols, :])
@@ -288,18 +284,14 @@
     hidden[...] = (coef * (pg * jax.nn.sigmoid(pg) * pu)).astype(jnp.bfloat16)
     lane = lax.broadcasted_iota(jnp.int32, side.shape, 1)
     side[...] = jnp.where(lane == 0, recip, jnp.where(lane == 1, coef, 0.0))
-
-
-def out_whole(hidden, wd, *refs):
-    parts = refs[:-2]
-    sums, sems = refs[-2:]
-    pending = []
+    for copy in pending:
+        copy.wait()
+
+
+def out_whole(hidden, wd, *parts):
     for k in range(wd.shape[1] // WIDE):
         cols = slice(k * WIDE, (k + 1) * WIDE)
-        sums[:, cols] = matmul(hidden[...], wd[:, cols]).astype(jnp.bfloat16)
-        pending += send_parts(sums, parts, cols, sems, k * len(parts))
-    for copy in pending:
-        copy.wait()
+        store_parts(parts, cols, matmul(hidden[...], wd[:, cols]).astype(jnp.bfloat16))
 
 
 def backward_whole(*refs, pieces, width, torus):
@@ -310,15 +302,20 @@
     outs = refs[7 + 2 * pieces :]
     og_all, pre_grads = outs[:2]
     parts = outs[2:-6]
-    acc, gate_s, up_s, sums, gain_ref, sems = outs[-6:]
-    pending = []
+    acc, gate_s, up_s, gain_ref, wd_s, sems = outs[-6:]
+    fetches = []
+    for k in range(width // WIDE):
+        cols = slice(k * WIDE, (k + 1) * WIDE)
+        fetches.append(pltpu.make_async_copy(wd.at[:, cols], wd_s.at[:, cols], sems.at[k]))
+        fetches[-1].start()
     steps = width // WIDE
     for k in range(steps):
         cols = slice(k * WIDE, (k + 1) * WIDE)
         for p, rows in enumerate(load_rows(grad, cols)):
             each = rows.shape[0]
             og_all[p * each : (p + 1) * each, cols] = rows.astype(jnp.bfloat16)
-        got = contract_cols(og_all[:, cols], wd[:, cols])
+        fetches[k].wait()
+        got = contract_cols(og_all[:, cols], wd_s[:, cols])
         if k == 0:
             acc[...] = got
         else:
@@ -330,7 +327,7 @@
     for k in range(steps):
         cols = slice(k * WIDE, (k + 1) * WIDE)
         back = contract_cols(gate_s[...], wg[cols, :]) + contract_cols(up_s[...], wu[cols, :])
-        sums[:, cols] = back.astype(jnp.bfloat16)
+        store_parts(parts, cols, back.astype(jnp.bfloat16))
         total = None
         for p, x in enumerate(load_rows(tok, cols)):
             each = x.shape[0]
@@ -338,12 +335,8 @@
             part = back[rows] * (x * recip[rows])
             total = part if p == 0 else total + part
         keep_gain(gain_ref, total, k * WIDE // META)
-        if k == steps - 1:
-            sums[:, width:] = gain_block(torus, spot, gain_ref, width, recip.shape[0])
-            cols = slice(k * WIDE, width + META)
-        pending += send_parts(sums, parts, cols, sems, steps + k * len(parts))
-    for copy in pending:
-        copy.wait()
+    block = gain_block(torus, spot, gain_ref, width, recip.shape[0])
+    store_parts(parts, slice(width, width + META), block)
 
 
 def keep_gain(gain_ref, total, first):
@@ -533,11 +526,8 @@
     return pltpu.CompilerParams(dimension_semantics=("arbitrary",), vmem_limit_bytes=mib * 2**20)
 
 
-def placed(shapes, low, high):
-    return [
-        (pltpu.VMEM if low <= k < high else pltpu.HBM)(s.shape, s.dtype)
-        for k, s in enumerate(shapes)
-    ]
+def placed(shapes):
+    return [pltpu.VMEM(s.shape, s.dtype) for s in shapes]
 
 
 def shapes_of(rows, width, hid, size, parts):
@@ -572,28 +562,28 @@
     fixed = lambda i: (0, 0)
     if rows <= WHOLE_ROWS:
         vmem = pl.BlockSpec(memory_space=pltpu.VMEM)
-        hbm = pl.BlockSpec(memory_space=pltpu.HBM)
         shapes = shapes_of(rows, width, hid, size, CORES * n3)
         outs = pl.pallas_call(
             functools.partial(forward_whole, pieces=pieces, width=width, top=top),
             in_specs=[pl.BlockSpec(memory_space=pltpu.SMEM)] * 2 + [vmem] * (pieces + 3),
-            out_specs=[vmem] * 5,
-            out_shape=placed(shapes[:5], 0, 5),
-            scratch_shapes=[pltpu.VMEM((rows, hid), jnp.float32)] * 2,
-            compiler_params=limit(8),
+            out_specs=[pl.BlockSpec(memory_space=pltpu.HBM)] + [vmem] * 4,
+            out_shape=[pltpu.HBM(shapes[0].shape, shapes[0].dtype)] + placed(shapes[1:5]),
+            scratch_shapes=[
+                pltpu.VMEM((rows, hid), jnp.float32),
+                pltpu.VMEM((rows, hid), jnp.float32),
+                pltpu.VMEM((rows, width), jnp.bfloat16),
+                pltpu.SemaphoreType.DMA((width // WIDE,)),
+            ],
+            compiler_params=limit(12),
             cost_estimate=cost(4 * rows * width * hid, 4 * width * hid + 4 * rows * width),
             name="forward",
         )(spot, ramp_step, *tok, gain, *on_chip(wg, wu))
         parts = pl.pallas_call(
             out_whole,
             in_specs=[vmem] * 2,
-            out_specs=[hbm] * (CORES * n3),
-            out_shape=placed(shapes[5:], 0, 0),
-            scratch_shapes=[
-                pltpu.VMEM((rows, width), jnp.bfloat16),
-                pltpu.SemaphoreType.DMA((width // WIDE * CORES * n3,)),
-            ],
-            compiler_params=limit(6),
+            out_specs=[vmem] * (CORES * n3),
+            out_shape=placed(shapes[5:]),
+            compiler_params=limit(5),
             cost_estimate=cost(2 * rows * width * hid, 2 * width * hid + 2 * rows * width),
             name="out",
         )(*on_chip(outs[3], wd))
@@ -651,24 +641,26 @@
     ] + [jax.ShapeDtypeStruct((size, width + META), jnp.bfloat16)] * (CORES * n3)
     if rows <= WHOLE_ROWS:
         vmem = pl.BlockSpec(memory_space=pltpu.VMEM)
-        hbm = pl.BlockSpec(memory_space=pltpu.HBM)
         outs = pl.pallas_call(
             functools.partial(backward_whole, pieces=pieces, width=width, torus=torus),
-            in_specs=[pl.BlockSpec(memory_space=pltpu.SMEM)] + [vmem] * (2 * pieces + 6),
-            out_specs=[vmem, vmem] + [hbm] * (CORES * n3),
-            out_shape=placed(shapes, 0, 2),
+            in_specs=[pl.BlockSpec(memory_space=pltpu.SMEM)]
+            + [vmem] * (2 * pieces)
+            + [pl.BlockSpec(memory_space=pltpu.HBM)]
+            + [vmem] * 5,
+            out_specs=[vmem] * (2 + CORES * n3),
+            out_shape=placed(shapes),
             scratch_shapes=[
                 pltpu.VMEM((rows, hid), jnp.float32),
                 pltpu.VMEM((rows, hid), jnp.bfloat16),
                 pltpu.VMEM((rows, hid), jnp.bfloat16),
-                pltpu.VMEM((rows, width + META), jnp.bfloat16),
                 pltpu.VMEM((width // META + 8, META), jnp.float32),
-                pltpu.SemaphoreType.DMA((width // WIDE * (1 + CORES * n3),)),
+                pltpu.VMEM((hid, width), jnp.bfloat16),
+                pltpu.SemaphoreType.DMA((width // WIDE,)),
             ],
-            compiler_params=limit(12),
+            compiler_params=limit(17),
             cost_estimate=cost(6 * rows * width * hid, 6 * width * hid + 6 * rows * width),
             name="backward",
-        )(spot, *grad, *tok, *on_chip(wd, wg, wu, pre_gate, pre_up, side))
+        )(spot, *grad, *tok, *off_chip(wd), *on_chip(wg, wu, pre_gate, pre_up, side))
         return (*outs[:2], [outs[2 + c * n3 : 2 + (c + 1) * n3] for c in range(CORES)])
     outs = pl.pallas_call(
         functools.partial(backward_kernel, pieces=pieces, steps=steps, width=width, torus=torus),
@@ -720,7 +712,7 @@
         compiler_params=params(20),
         cost_estimate=cost(4 * rows * width * hid, 4 * width * hid + 2 * rows * width),
         name="up_grads",
-    )(*(on_chip(scaled, pre_grads) if rows <= WHOLE_ROWS else (scaled, pre_grads)))
+    )(scaled, pre_grads)
 
 
 def down_grad(hidden, og_all):
@@ -769,7 +761,7 @@
     og_all, pre_grads, parts = backward(torus, spot, grad, tok, wd, wg, wu, pre_gate, pre_up, side)
     w_gate_grad, w_up_grad = up_grads(scaled, pre_grads)
     w_down_grad = down_grad(hidden, og_all)
-    mixed, w_down_grad = scatter_sum(torus, out_parts, w_down_grad)
+    mixed, w_gate_grad = scatter_sum(torus, out_parts, w_gate_grad)
     mixed = mixed.astype(jnp.bfloat16)
     total = scatter_sum(torus, parts)
     normed_grad = total[:, :width]

time: 147 us -> 147 us (level)
  no operation moved by 1% of the time
where the time goes in v2:
time: 147 us
  waiting for transfers between devices  63 us (43%)
  starting transfers between devices  41.3 us (28%)
  Pallas kernels  36.5 us (25%)
  other arithmetic  3.15 us (2%)
  local copies, waits for them, and re-layouts  1.68 us (1%)
    ppermute x44, waiting for transfers between devices, shift_rows(): return lax.ppermute(rows, AXES, torus.pairs(step, shift))  63 us
    ppermute x44, starting transfers between devices, shift_rows(): return lax.ppermute(rows, AXES, torus.pairs(step, shift))  41.3 us
    pallas_call x1, Pallas kernels, backward(): pl.pallas_call(functools.partial(backward_whole, pieces=pieces, width=wid...  9.32 us
    pallas_call x2, Pallas kernels, prefetch(): pl.pallas_call(prefetch_kernel, in_specs=[pl.BlockSpec(memory_space=pltpu...  7.26 us
    pallas_call x1, Pallas kernels, up_grads(): pl.pallas_call(up_grads_kernel, grid=(width // step,), in_specs=[pl.Block...  6.35 us
    pallas_call x1, Pallas kernels, forward(): pl.pallas_call(functools.partial(forward_whole, pieces=pieces, width=widt...  5.69 us
    pallas_call x1, Pallas kernels, down_grad(): pl.pallas_call(down_grad_kernel, grid=(width // step,), in_specs=[pl.Bloc...  4.71 us
  transfers between devices with their start and end apart: 44, of which 12 were waited for; matrix products, arithmetic and copies ran while one was open for 2% of the time, Pallas kernels for 25%

profile of v2, /device:TPU:0, one launch (start us, length us, event | category | flops | bytes accessed | tf_op | source)
XLA Modules:
  0.0 146.5 jit_solution(2609914882100543249)
XLA Ops:
  0.6 3.1 %collective-permute-start.29 = (bf16[8,7168]{1,0:T(8,128)(2,1)}, bf16[8,7168]{1,0:T(8,128)(2,1)S(1)}, u32[]{:S(2)}, u32[]{:S(2)}) collective-permute-start(bf16[8,7168]{1,0:T(8,128)(2,1)} %param.10), channel_id=1, source_target_pairs={{0,2},{1,17},{2,0},{3,19},{4,6},{5,21},{6,4},{7,23},{8,10},{9,25},... | collective-permute-start | bytes 344072 | tf_op jit(solution)/shard_map/ppermute | solution.py:83
  3.7 3.6 %collective-permute-start.21 = (bf16[8,7168]{1,0:T(8,128)(2,1)}, bf16[8,7168]{1,0:T(8,128)(2,1)S(1)}, u32[]{:S(2)}, u32[]{:S(2)}) collective-permute-start(bf16[8,7168]{1,0:T(8,128)(2,1)} %param.10), channel_id=1, source_target_pairs={{0,12},{1,13},{2,14},{3,15},{4,8},{5,9},{6,10},{7,11},{8,4},{9,5},... | collective-permute-start | bytes 344072 | tf_op jit(solution)/shard_map/ppermute | solution.py:83
  10.6 3.6 %prefetch.2.refs_13_.refs_22_ = bf16[7168,512]{1,0:T(8,128)(2,1)S(1)} custom-call(u32[3]{0:T(128)S(1)} %pad_add_fusion._.refs_0_, bf16[7168,512]{1,0:T(8,128)(2,1)} %bitcast.17), custom_call_target="tpu_custom_call" | custom-call | tf_op jit(solution)/shard_map/prefetch/pallas_call | solution.py:375
  14.3 3.6 %prefetch.3.refs_14_.refs_23_ = bf16[7168,512]{1,0:T(8,128)(2,1)S(1)} custom-call(u32[3]{0:T(128)S(1)} %pad_add_fusion._.refs_0_, bf16[7168,512]{1,0:T(8,128)(2,1)} %bitcast.18), custom_call_target="tpu_custom_call" | custom-call | tf_op jit(solution)/shard_map/prefetch/pallas_call | solution.py:375
  19.4 3.6 %collective-permute-start.2 = (bf16[8,7296]{1,0:T(8,128)(2,1)S(1)}, bf16[8,7296]{1,0:T(8,128)(2,1)S(1)}, u32[]{:S(2)}, u32[]{:S(2)}) collective-permute-start(bf16[8,7296]{1,0:T(8,128)(2,1)S(1)} %pack.1), channel_id=1, source_target_pairs={{0,12},{1,13},{2,14},{3,15},{4,8},{5,9},{6,10},{7,11},{8,4},{9,5},... | collective-permute-start | bytes 350216 | tf_op jit(solution)/shard_map/ppermute | solution.py:83
  23.9 2.6 %collective-permute-done.2.refs_2_ = bf16[8,7296]{1,0:T(8,128)(2,1)S(1)} collective-permute-done((bf16[8,7296]{1,0:T(8,128)(2,1)S(1)}, bf16[8,7296]{1,0:T(8,128)(2,1)S(1)}, u32[]{:S(2)}, u32[]{:S(2)}) %collective-permute-start.2) | collective-permute-done | bytes 116768 | tf_op jit(solution)/shard_map/ppermute | solution.py:83
  27.6 3.6 %collective-permute-done.1.refs_1_ = bf16[8,7296]{1,0:T(8,128)(2,1)S(1)} collective-permute-done((bf16[8,7296]{1,0:T(8,128)(2,1)S(1)}, bf16[8,7296]{1,0:T(8,128)(2,1)S(1)}, u32[]{:S(2)}, u32[]{:S(2)}) %collective-permute-start.1) | collective-permute-done | bytes 116768 | tf_op jit(solution)/shard_map/ppermute | solution.py:83
  33.8 1.5 %collective-permute-start.12 = (bf16[8,7296]{1,0:T(8,128)(2,1)S(1)}, bf16[8,7296]{1,0:T(8,128)(2,1)S(1)}, u32[]{:S(2)}, u32[]{:S(2)}) collective-permute-start(bf16[8,7296]{1,0:T(8,128)(2,1)S(1)} %collective-permute-done.10), channel_id=1, source_target_pairs={{0,16},{1,3},{2,18},{3,1},{4,20},{5,7},{6,22},{7,5},{8,24},{9,11},... | collective-permute-start | bytes 350216 | tf_op jit(solution)/shard_map/ppermute | solution.py:83
  35.3 1.6 %collective-permute-start.22 = (bf16[24,7168]{1,0:T(8,128)(2,1)S(1)}, bf16[24,7168]{1,0:T(8,128)(2,1)S(1)}, u32[]{:S(2)}, u32[]{:S(2)}) collective-permute-start(bf16[24,7168]{1,0:T(8,128)(2,1)S(1)} %join.3.refs_1_), channel_id=1, source_target_pairs={{0,2},{1,17},{2,0},{3,19},{4,6},{5,21},{6,4},{7,23},{8,10},{9,25},... | collective-permute-start | bytes 1032200 | tf_op jit(solution)/shard_map/ppermute | solution.py:83
  36.9 7.6 %collective-permute-done.31 = bf16[8,7168]{1,0:T(8,128)(2,1)S(1)} collective-permute-done((bf16[8,7168]{1,0:T(8,128)(2,1)S(1)}, bf16[8,7168]{1,0:T(8,128)(2,1)S(1)}, u32[]{:S(2)}, u32[]{:S(2)}) %collective-permute-start.31) | collective-permute-done | bytes 114720 | tf_op jit(solution)/shard_map/ppermute | solution.py:83
  44.6 2.5 %collective-permute-done.12 = bf16[8,7296]{1,0:T(8,128)(2,1)S(1)} collective-permute-done((bf16[8,7296]{1,0:T(8,128)(2,1)S(1)}, bf16[8,7296]{1,0:T(8,128)(2,1)S(1)}, u32[]{:S(2)}, u32[]{:S(2)}) %collective-permute-start.12) | collective-permute-done | bytes 116768 | tf_op jit(solution)/shard_map/ppermute | solution.py:83
  47.1 1.5 %collective-permute-start.4 = (bf16[24,7296]{1,0:T(8,128)(2,1)S(1)}, bf16[24,7296]{1,0:T(8,128)(2,1)S(1)}, u32[]{:S(2)}, u32[]{:S(2)}) collective-permute-start(bf16[24,7296]{1,0:T(8,128)(2,1)S(1)} %join.2.refs_2_.refs_11_), channel_id=1, source_target_pairs={{0,16},{1,3},{2,18},{3,1},{4,20},{5,7},{6,22},{7,5},{8,24},{9,11},... | collective-permute-start | bytes 1050632 | tf_op jit(solution)/shard_map/ppermute | solution.py:83
  49.2 1.6 %collective-permute-start.24 = (bf16[24,7168]{1,0:T(8,128)(2,1)S(1)}, bf16[24,7168]{1,0:T(8,128)(2,1)S(1)}, u32[]{:S(2)}, u32[]{:S(2)}) collective-permute-start(bf16[24,7168]{1,0:T(8,128)(2,1)S(1)} %collective-permute-done.22.refs_2_), channel_id=1, source_target_pairs={{0,16},{1,3},{2,18},{3,1},{4,20},{5,7},{6,22},{7,5},{8,24},{9,11},... | collective-permute-start | bytes 1032200 | tf_op jit(solution)/shard_map/ppermute | solution.py:83
  50.8 3.6 %collective-permute-done.4.refs_4_.refs_13_ = bf16[24,7296]{1,0:T(8,128)(2,1)S(1)} collective-permute-done((bf16[24,7296]{1,0:T(8,128)(2,1)S(1)}, bf16[24,7296]{1,0:T(8,128)(2,1)S(1)}, u32[]{:S(2)}, u32[]{:S(2)}) %collective-permute-start.4) | collective-permute-done | bytes 350240 | tf_op jit(solution)/shard_map/ppermute | solution.py:83
  54.4 3.7 %collective-permute-done.5.refs_5_.refs_14_ = bf16[24,7296]{1,0:T(8,128)(2,1)S(1)} collective-permute-done((bf16[24,7296]{1,0:T(8,128)(2,1)S(1)}, bf16[24,7296]{1,0:T(8,128)(2,1)S(1)}, u32[]{:S(2)}, u32[]{:S(2)}) %collective-permute-start.5) | collective-permute-done | bytes 350240 | tf_op jit(solution)/shard_map/ppermute | solution.py:83
  58.7 3.1 %collective-permute-done.24.refs_4_ = bf16[24,7168]{1,0:T(8,128)(2,1)S(1)} collective-permute-done((bf16[24,7168]{1,0:T(8,128)(2,1)S(1)}, bf16[24,7168]{1,0:T(8,128)(2,1)S(1)}, u32[]{:S(2)}, u32[]{:S(2)}) %collective-permute-start.24) | collective-permute-done | bytes 344096 | tf_op jit(solution)/shard_map/ppermute | solution.py:83
  62.9 5.7 %forward.1 = (bf16[256,7168]{1,0:T(8,128)(2,1)}, f32[256,512]{1,0:T(8,128)S(1)}, f32[256,512]{1,0:T(8,128)S(1)}, bf16[256,512]{1,0:T(8,128)(2,1)S(1)}, f32[256,128]{1,0:T(8,128)S(1)}) custom-call(u32[3]{0:T(128)S(1)} %pad_add_fusion._.refs_0_, s32[16]{0:T(128)S(1)} %copy-done.1, bf16[24,7296]{1,0:T(8,128)(2,1)S(1)} %join.2.refs_2_.refs_11_, ...), custom_call_target="tpu_custom_call" | custom-call | flops 3758096384 | bytes 22020096 | tf_op jit(solution)/shard_map/forward/pallas_call | solution.py:566
  68.6 2.1 %out.1 = (bf16[64,7168]{1,0:T(8,128)(2,1)S(1)}, bf16[64,7168]{1,0:T(8,128)(2,1)S(1)}, bf16[64,7168]{1,0:T(8,128)(2,1)S(1)}, bf16[64,7168]{1,0:T(8,128)(2,1)S(1)}) custom-call(bf16[256,512]{1,0:T(8,128)(2,1)S(1)} %get-tuple-element.25.hidden, bf16[512,7168]{1,0:T(8,128)(2,1)S(1)} %bitcast.15), custom_call_target="tpu_custom_call" | custom-call | flops 1879048192 | bytes 11010048 | tf_op jit(solution)/shard_map/out/pallas_call | solution.py:581
  70.8 9.3 %backward.1 = (bf16[256,7168]{1,0:T(8,128)(2,1)S(1)}, bf16[256,1024]{1,0:T(8,128)(2,1)S(1)}, bf16[64,7296]{1,0:T(8,128)(2,1)S(1)}, bf16[64,7296]{1,0:T(8,128)(2,...) custom-call(u32[3]{0:T(128)S(1)} %pad_add_fusion._.refs_0_, bf16[24,7168]{1,0:T(8,128)(2,1)S(1)} %join.3.refs_1_, ...), custom_call_target="tpu_custom_call" | custom-call | flops 5637144576 | bytes 33030144 | tf_op jit(solution)/shard_map/backward/pallas_call | solution.py:644
  81.2 4.7 %down_grad.1 = bf16[512,7168]{1,0:T(8,128)(2,1)} custom-call(bf16[256,512]{1,0:T(8,128)(2,1)S(1)} %get-tuple-element.25.hidden, bf16[256,7168]{1,0:T(8,128)(2,1)S(1)} %get-tuple-element.43.og_all), custom_call_target="tpu_custom_call" | custom-call | flops 1879048192 | bytes 11010048 | tf_op jit(solution)/shard_map/down_grad/pallas_call | solution.py:722
  85.9 6.3 %up_grads.1 = (bf16[7168,512]{1,0:T(8,128)(2,1)}, bf16[7168,512]{1,0:T(8,128)(2,1)}) custom-call(bf16[256,7168]{1,0:T(8,128)(2,1)S(1)} %copy-done.2, bf16[256,1024]{1,0:T(8,128)(2,1)S(1)} %get-tuple-element.34.pre_grads), custom_call_target="tpu_custom_call" | custom-call | flops 3758096384 | bytes 18350080 | tf_op jit(solution)/shard_map/up_grads/pallas_call | solution.py:703
  92.5 1.6 %collective-permute-start.16 = (bf16[32,7168]{1,0:T(8,128)(2,1)S(1)}, bf16[32,7168]{1,0:T(8,128)(2,1)S(1)}, u32[]{:S(2)}, u32[]{:S(2)}) collective-permute-start(bf16[32,7168]{1,0:T(8,128)(2,1)S(1)} %get-tuple-element.52), channel_id=1, source_target_pairs={{0,16},{1,3},{2,18},{3,1},{4,20},{5,7},{6,22},{7,5},{8,24},{9,11},... | collective-permute-start | bytes 1376264 | tf_op jit(solution)/shard_map/ppermute | solution.py:83
  94.8 1.6 %collective-permute-start.38 = (bf16[32,7296]{1,0:T(8,128)(2,1)S(1)}, bf16[32,7296]{1,0:T(8,128)(2,1)S(1)}, u32[]{:S(2)}, u32[]{:S(2)}) collective-permute-start(bf16[32,7296]{1,0:T(8,128)(2,1)S(1)} %get-tuple-element.50), channel_id=1, source_target_pairs={{0,16},{1,3},{2,18},{3,1},{4,20},{5,7},{6,22},{7,5},{8,24},{9,11},... | collective-permute-start | bytes 1400840 | tf_op jit(solution)/shard_map/ppermute | solution.py:83
  96.9 9.0 %collective-permute-done.17 = bf16[32,7168]{1,0:T(8,128)(2,1)S(1)} collective-permute-done((bf16[32,7168]{1,0:T(8,128)(2,1)S(1)}, bf16[32,7168]{1,0:T(8,128)(2,1)S(1)}, u32[]{:S(2)}, u32[]{:S(2)}) %collective-permute-start.17) | collective-permute-done | bytes 458784 | tf_op jit(solution)/shard_map/ppermute | solution.py:83
  106.7 14.2 %collective-permute-done.39 = bf16[32,7296]{1,0:T(8,128)(2,1)S(1)} collective-permute-done((bf16[32,7296]{1,0:T(8,128)(2,1)S(1)}, bf16[32,7296]{1,0:T(8,128)(2,1)S(1)}, u32[]{:S(2)}, u32[]{:S(2)}) %collective-permute-start.39) | collective-permute-done | bytes 466976 | tf_op jit(solution)/shard_map/ppermute | solution.py:83
  121.9 2.3 %collective-permute-start.33 = (bf16[8,7168]{1,0:T(8,128)(2,1)S(1)}, bf16[8,7168]{1,0:T(8,128)(2,1)S(1)}, u32[]{:S(2)}, u32[]{:S(2)}) collective-permute-start(bf16[8,7168]{1,0:T(8,128)(2,1)S(1)} %get-tuple-element.57), channel_id=1, source_target_pairs={{0,12},{1,13},{2,14},{3,15},{4,8},{5,9},{6,10},{7,11},{8,4},{9,5},... | collective-permute-start | bytes 344072 | tf_op jit(solution)/shard_map/ppermute | solution.py:83
  124.2 2.2 %collective-permute-start.34 = (bf16[8,7168]{1,0:T(8,128)(2,1)S(1)}, bf16[8,7168]{1,0:T(8,128)(2,1)S(1)}, u32[]{:S(2)}, u32[]{:S(2)}) collective-permute-start(bf16[8,7168]{1,0:T(8,128)(2,1)S(1)} %get-tuple-element.59), channel_id=1, source_target_pairs={{0,8},{1,9},{2,10},{3,11},{4,12},{5,13},{6,14},{7,15},{8,0},{9,1},... | collective-permute-start | bytes 344072 | tf_op jit(solution)/shard_map/ppermute | solution.py:83
  126.4 3.4 %collective-permute-done.40 = bf16[32,7296]{1,0:T(8,128)(2,1)S(1)} collective-permute-done((bf16[32,7296]{1,0:T(8,128)(2,1)S(1)}, bf16[32,7296]{1,0:T(8,128)(2,1)S(1)}, u32[]{:S(2)}, u32[]{:S(2)}) %collective-permute-start.40) | collective-permute-done | bytes 466976 | tf_op jit(solution)/shard_map/ppermute | solution.py:83
  130.0 2.3 %collective-permute-start.41 = (bf16[8,7296]{1,0:T(8,128)(2,1)S(1)}, bf16[8,7296]{1,0:T(8,128)(2,1)S(1)}, u32[]{:S(2)}, u32[]{:S(2)}) collective-permute-start(bf16[8,7296]{1,0:T(8,128)(2,1)S(1)} %get-tuple-element.54), channel_id=1, source_target_pairs={{0,12},{1,13},{2,14},{3,15},{4,8},{5,9},{6,10},{7,11},{8,4},{9,5},... | collective-permute-start | bytes 350216 | tf_op jit(solution)/shard_map/ppermute | solution.py:83
  132.4 2.0 %collective-permute-start.42 = (bf16[8,7296]{1,0:T(8,128)(2,1)S(1)}, bf16[8,7296]{1,0:T(8,128)(2,1)S(1)}, u32[]{:S(2)}, u32[]{:S(2)}) collective-permute-start(bf16[8,7296]{1,0:T(8,128)(2,1)S(1)} %get-tuple-element.56), channel_id=1, source_target_pairs={{0,8},{1,9},{2,10},{3,11},{4,12},{5,13},{6,14},{7,15},{8,0},{9,1},... | collective-permute-start | bytes 350216 | tf_op jit(solution)/shard_map/ppermute | solution.py:83
  134.5 4.9 %collective-permute-done.34 = bf16[8,7168]{1,0:T(8,128)(2,1)S(1)} collective-permute-done((bf16[8,7168]{1,0:T(8,128)(2,1)S(1)}, bf16[8,7168]{1,0:T(8,128)(2,1)S(1)}, u32[]{:S(2)}, u32[]{:S(2)}) %collective-permute-start.34) | collective-permute-done | bytes 114720 | tf_op jit(solution)/shard_map/ppermute | solution.py:83
  140.1 4.7 %collective-permute-done.42 = bf16[8,7296]{1,0:T(8,128)(2,1)S(1)} collective-permute-done((bf16[8,7296]{1,0:T(8,128)(2,1)S(1)}, bf16[8,7296]{1,0:T(8,128)(2,1)S(1)}, u32[]{:S(2)}, u32[]{:S(2)}) %collective-permute-start.42) | collective-permute-done | bytes 116768 | tf_op jit(solution)/shard_map/ppermute | solution.py:83
  (100 shorter events, 18.9 us)
Async XLA Ops:
  0.6 18.3 %collective-permute-start.29 = (bf16[8,7168]{1,0:T(8,128)(2,1)}, bf16[8,7168]{1,0:T(8,128)(2,1)S(1)}, u32[]{:S(2)}, u32[]{:S(2)}) collective-permute-start(bf16[8,7168]{1,0:T(8,128)(2,1)} %param.10), channel_id=1, source_target_pairs={{0,2},{1,17},{2,0},{3,19},{4,6},{5,21},{6,4},{7,23},{8,10},{9,25},... | collective-permute-start | bytes 344072 | tf_op jit(solution)/shard_map/ppermute | solution.py:83
  3.7 15.7 %collective-permute-start.21 = (bf16[8,7168]{1,0:T(8,128)(2,1)}, bf16[8,7168]{1,0:T(8,128)(2,1)S(1)}, u32[]{:S(2)}, u32[]{:S(2)}) collective-permute-start(bf16[8,7168]{1,0:T(8,128)(2,1)} %param.10), channel_id=1, source_target_pairs={{0,12},{1,13},{2,14},{3,15},{4,8},{5,9},{6,10},{7,11},{8,4},{9,5},... | collective-permute-start | bytes 344072 | tf_op jit(solution)/shard_map/ppermute | solution.py:83
  7.3 15.7 %collective-permute-start.20 = (bf16[8,7168]{1,0:T(8,128)(2,1)}, bf16[8,7168]{1,0:T(8,128)(2,1)S(1)}, u32[]{:S(2)}, u32[]{:S(2)}) collective-permute-start(bf16[8,7168]{1,0:T(8,128)(2,1)} %param.10), channel_id=1, source_target_pairs={{0,8},{1,9},{2,10},{3,11},{4,12},{5,13},{6,14},{7,15},{8,0},{9,1},... | collective-permute-start | bytes 344072 | tf_op jit(solution)/shard_map/ppermute | solution.py:83
  7.3 15.7 %collective-permute-start.19 = (bf16[8,7168]{1,0:T(8,128)(2,1)}, bf16[8,7168]{1,0:T(8,128)(2,1)S(1)}, u32[]{:S(2)}, u32[]{:S(2)}) collective-permute-start(bf16[8,7168]{1,0:T(8,128)(2,1)} %param.10), channel_id=1, source_target_pairs={{0,4},{1,5},{2,6},{3,7},{4,0},{5,1},{6,2},{7,3},{8,12},{9,13},{10,... | collective-permute-start | bytes 344072 | tf_op jit(solution)/shard_map/ppermute | solution.py:83
  8.1 25.2 %collective-permute-start.30 = (bf16[8,7168]{1,0:T(8,128)(2,1)}, bf16[8,7168]{1,0:T(8,128)(2,1)S(1)}, u32[]{:S(2)}, u32[]{:S(2)}) collective-permute-start(bf16[8,7168]{1,0:T(8,128)(2,1)} %param.10), channel_id=1, source_target_pairs={{0,16},{1,3},{2,18},{3,1},{4,20},{5,7},{6,22},{7,5},{8,24},{9,11},... | collective-permute-start | bytes 344072 | tf_op jit(solution)/shard_map/ppermute | solution.py:83
  18.9 14.9 %collective-permute-start.10 = (bf16[8,7296]{1,0:T(8,128)(2,1)S(1)}, bf16[8,7296]{1,0:T(8,128)(2,1)S(1)}, u32[]{:S(2)}, u32[]{:S(2)}) collective-permute-start(bf16[8,7296]{1,0:T(8,128)(2,1)S(1)} %pack.1), channel_id=1, source_target_pairs={{0,2},{1,17},{2,0},{3,19},{4,6},{5,21},{6,4},{7,23},{8,10},{9,25},... | collective-permute-start | bytes 350216 | tf_op jit(solution)/shard_map/ppermute | solution.py:83
  23.0 9.6 %collective-permute-start = (bf16[8,7296]{1,0:T(8,128)(2,1)S(1)}, bf16[8,7296]{1,0:T(8,128)(2,1)S(1)}, u32[]{:S(2)}, u32[]{:S(2)}) collective-permute-start(bf16[8,7296]{1,0:T(8,128)(2,1)S(1)} %pack.1), channel_id=1, source_target_pairs={{0,4},{1,5},{2,6},{3,7},{4,0},{5,1},{6,2},{7,3},{8,12},{9,13},{10,... | collective-permute-start | bytes 350216 | tf_op jit(solution)/shard_map/ppermute | solution.py:83
  31.2 18.0 %collective-permute-start.23 = (bf16[24,7168]{1,0:T(8,128)(2,1)S(1)}, bf16[24,7168]{1,0:T(8,128)(2,1)S(1)}, u32[]{:S(2)}, u32[]{:S(2)}) collective-permute-start(bf16[24,7168]{1,0:T(8,128)(2,1)S(1)} %join.3.refs_1_), channel_id=1, source_target_pairs={{0,16},{1,3},{2,18},{3,1},{4,20},{5,7},{6,22},{7,5},{8,24},{9,11},... | collective-permute-start | bytes 1032200 | tf_op jit(solution)/shard_map/ppermute | solution.py:83
  32.7 11.9 %collective-permute-start.31 = (bf16[8,7168]{1,0:T(8,128)(2,1)S(1)}, bf16[8,7168]{1,0:T(8,128)(2,1)S(1)}, u32[]{:S(2)}, u32[]{:S(2)}) collective-permute-start(bf16[8,7168]{1,0:T(8,128)(2,1)S(1)} %collective-permute-done.29), channel_id=1, source_target_pairs={{0,16},{1,3},{2,18},{3,1},{4,20},{5,7},{6,22},{7,5},{8,24},{9,11},... | collective-permute-start | bytes 344072 | tf_op jit(solution)/shard_map/ppermute | solution.py:83
  33.2 15.3 %collective-permute-start.3 = (bf16[24,7296]{1,0:T(8,128)(2,1)S(1)}, bf16[24,7296]{1,0:T(8,128)(2,1)S(1)}, u32[]{:S(2)}, u32[]{:S(2)}) collective-permute-start(bf16[24,7296]{1,0:T(8,128)(2,1)S(1)} %join.2.refs_2_.refs_11_), channel_id=1, source_target_pairs={{0,2},{1,17},{2,0},{3,19},{4,6},{5,21},{6,4},{7,23},{8,10},{9,25},... | collective-permute-start | bytes 1050632 | tf_op jit(solution)/shard_map/ppermute | solution.py:83
  33.8 13.2 %collective-permute-start.12 = (bf16[8,7296]{1,0:T(8,128)(2,1)S(1)}, bf16[8,7296]{1,0:T(8,128)(2,1)S(1)}, u32[]{:S(2)}, u32[]{:S(2)}) collective-permute-start(bf16[8,7296]{1,0:T(8,128)(2,1)S(1)} %collective-permute-done.10), channel_id=1, source_target_pairs={{0,16},{1,3},{2,18},{3,1},{4,20},{5,7},{6,22},{7,5},{8,24},{9,11},... | collective-permute-start | bytes 350216 | tf_op jit(solution)/shard_map/ppermute | solution.py:83
  35.3 13.9 %collective-permute-start.22 = (bf16[24,7168]{1,0:T(8,128)(2,1)S(1)}, bf16[24,7168]{1,0:T(8,128)(2,1)S(1)}, u32[]{:S(2)}, u32[]{:S(2)}) collective-permute-start(bf16[24,7168]{1,0:T(8,128)(2,1)S(1)} %join.3.refs_1_), channel_id=1, source_target_pairs={{0,2},{1,17},{2,0},{3,19},{4,6},{5,21},{6,4},{7,23},{8,10},{9,25},... | collective-permute-start | bytes 1032200 | tf_op jit(solution)/shard_map/ppermute | solution.py:83
  48.6 9.6 %collective-permute-start.5 = (bf16[24,7296]{1,0:T(8,128)(2,1)S(1)}, bf16[24,7296]{1,0:T(8,128)(2,1)S(1)}, u32[]{:S(2)}, u32[]{:S(2)}) collective-permute-start(bf16[24,7296]{1,0:T(8,128)(2,1)S(1)} %collective-permute-done.3.refs_3_.refs_12_), channel_id=1, source_target_pairs={{0,16},{1,3},{2,18},{3,1},{4,20},{5,7},{6,22},{7,5},{8,24},{9,11},... | collective-permute-start | bytes 1050632 | tf_op jit(solution)/shard_map/ppermute | solution.py:83
  49.2 9.0 %collective-permute-start.13 = (bf16[32,7296]{1,0:T(8,128)(2,1)S(1)}, bf16[32,7296]{1,0:T(8,128)(2,1)S(1)}, u32[]{:S(2)}, u32[]{:S(2)}) collective-permute-start(bf16[32,7296]{1,0:T(8,128)(2,1)S(1)} %pad_maximum_fusion.refs_10_.refs_19_), channel_id=1, source_target_pairs={{0,1},{1,0},{2,3},{3,2},{4,5},{5,4},{6,7},{7,6},{8,9},{9,8},{10,11... | collective-permute-start | bytes 1400840 | tf_op jit(solution)/shard_map/ppermute | solution.py:83
  49.2 12.6 %collective-permute-start.24 = (bf16[24,7168]{1,0:T(8,128)(2,1)S(1)}, bf16[24,7168]{1,0:T(8,128)(2,1)S(1)}, u32[]{:S(2)}, u32[]{:S(2)}) collective-permute-start(bf16[24,7168]{1,0:T(8,128)(2,1)S(1)} %collective-permute-done.22.refs_2_), channel_id=1, source_target_pairs={{0,16},{1,3},{2,18},{3,1},{4,20},{5,7},{6,22},{7,5},{8,24},{9,11},... | collective-permute-start | bytes 1032200 | tf_op jit(solution)/shard_map/ppermute | solution.py:83
  50.8 11.5 %collective-permute-start.7 = (bf16[24,7296]{1,0:T(8,128)(2,1)S(1)}, bf16[24,7296]{1,0:T(8,128)(2,1)S(1)}, u32[]{:S(2)}, u32[]{:S(2)}) collective-permute-start(bf16[24,7296]{1,0:T(8,128)(2,1)S(1)} %collective-permute-done.3.refs_3_.refs_12_), channel_id=1, source_target_pairs={{0,1},{1,0},{2,3},{3,2},{4,5},{5,4},{6,7},{7,6},{8,9},{9,8},{10,11... | collective-permute-start | bytes 1050632 | tf_op jit(solution)/shard_map/ppermute | solution.py:83
  58.2 12.5 %collective-permute-start.25 = (bf16[24,7168]{1,0:T(8,128)(2,1)S(1)}, bf16[24,7168]{1,0:T(8,128)(2,1)S(1)}, u32[]{:S(2)}, u32[]{:S(2)}) collective-permute-start(bf16[24,7168]{1,0:T(8,128)(2,1)S(1)} %join.3.refs_1_), channel_id=1, source_target_pairs={{0,1},{1,0},{2,3},{3,2},{4,5},{5,4},{6,7},{7,6},{8,9},{9,8},{10,11... | collective-permute-start | bytes 1032200 | tf_op jit(solution)/shard_map/ppermute | solution.py:83
  61.8 9.0 %collective-permute-start.26 = (bf16[24,7168]{1,0:T(8,128)(2,1)S(1)}, bf16[24,7168]{1,0:T(8,128)(2,1)S(1)}, u32[]{:S(2)}, u32[]{:S(2)}) collective-permute-start(bf16[24,7168]{1,0:T(8,128)(2,1)S(1)} %collective-permute-done.22.refs_2_), channel_id=1, source_target_pairs={{0,1},{1,0},{2,3},{3,2},{4,5},{5,4},{6,7},{7,6},{8,9},{9,8},{10,11... | collective-permute-start | bytes 1032200 | tf_op jit(solution)/shard_map/ppermute | solution.py:83
  70.7 21.6 %collective-permute-start.15 = (bf16[64,7168]{1,0:T(8,128)(2,1)S(1)}, bf16[64,7168]{1,0:T(8,128)(2,1)S(1)}, u32[]{:S(2)}, u32[]{:S(2)}) collective-permute-start(bf16[64,7168]{1,0:T(8,128)(2,1)S(1)} %get-tuple-element.29), channel_id=1, source_target_pairs={{0,1},{1,0},{2,3},{3,2},{4,5},{5,4},{6,7},{7,6},{8,9},{9,8},{10,11... | collective-permute-start | bytes 2752520 | tf_op jit(solution)/shard_map/ppermute | solution.py:83
  80.2 26.5 %collective-permute-start.36 = (bf16[64,7296]{1,0:T(8,128)(2,1)S(1)}, bf16[64,7296]{1,0:T(8,128)(2,1)S(1)}, u32[]{:S(2)}, u32[]{:S(2)}) collective-permute-start(bf16[64,7296]{1,0:T(8,128)(2,1)S(1)} %get-tuple-element.38), channel_id=1, source_target_pairs={{0,1},{1,0},{2,3},{3,2},{4,5},{5,4},{6,7},{7,6},{8,9},{9,8},{10,11... | collective-permute-start | bytes 2801672 | tf_op jit(solution)/shard_map/ppermute | solution.py:83
  80.7 13.9 %collective-permute-start.37 = (bf16[64,7296]{1,0:T(8,128)(2,1)S(1)}, bf16[64,7296]{1,0:T(8,128)(2,1)S(1)}, u32[]{:S(2)}, u32[]{:S(2)}) collective-permute-start(bf16[64,7296]{1,0:T(8,128)(2,1)S(1)} %get-tuple-element.40), channel_id=1, source_target_pairs={{0,1},{1,0},{2,3},{3,2},{4,5},{5,4},{6,7},{7,6},{8,9},{9,8},{10,11... | collective-permute-start | bytes 2801672 | tf_op jit(solution)/shard_map/ppermute | solution.py:83
  80.8 15.6 %collective-permute-start.14 = (bf16[64,7168]{1,0:T(8,128)(2,1)S(1)}, bf16[64,7168]{1,0:T(8,128)(2,1)S(1)}, u32[]{:S(2)}, u32[]{:S(2)}) collective-permute-start(bf16[64,7168]{1,0:T(8,128)(2,1)S(1)} %get-tuple-element.27), channel_id=1, source_target_pairs={{0,1},{1,0},{2,3},{3,2},{4,5},{5,4},{6,7},{7,6},{8,9},{9,8},{10,11... | collective-permute-start | bytes 2752520 | tf_op jit(solution)/shard_map/ppermute | solution.py:83
  92.5 29.2 %collective-permute-start.16 = (bf16[32,7168]{1,0:T(8,128)(2,1)S(1)}, bf16[32,7168]{1,0:T(8,128)(2,1)S(1)}, u32[]{:S(2)}, u32[]{:S(2)}) collective-permute-start(bf16[32,7168]{1,0:T(8,128)(2,1)S(1)} %get-tuple-element.52), channel_id=1, source_target_pairs={{0,16},{1,3},{2,18},{3,1},{4,20},{5,7},{6,22},{7,5},{8,24},{9,11},... | collective-permute-start | bytes 1376264 | tf_op jit(solution)/shard_map/ppermute | solution.py:83
  94.1 11.9 %collective-permute-start.17 = (bf16[32,7168]{1,0:T(8,128)(2,1)S(1)}, bf16[32,7168]{1,0:T(8,128)(2,1)S(1)}, u32[]{:S(2)}, u32[]{:S(2)}) collective-permute-start(bf16[32,7168]{1,0:T(8,128)(2,1)S(1)} %get-tuple-element.53), channel_id=1, source_target_pairs={{0,16},{1,3},{2,18},{3,1},{4,20},{5,7},{6,22},{7,5},{8,24},{9,11},... | collective-permute-start | bytes 1376264 | tf_op jit(solution)/shard_map/ppermute | solution.py:83
  94.8 31.6 %collective-permute-start.38 = (bf16[32,7296]{1,0:T(8,128)(2,1)S(1)}, bf16[32,7296]{1,0:T(8,128)(2,1)S(1)}, u32[]{:S(2)}, u32[]{:S(2)}) collective-permute-start(bf16[32,7296]{1,0:T(8,128)(2,1)S(1)} %get-tuple-element.50), channel_id=1, source_target_pairs={{0,16},{1,3},{2,18},{3,1},{4,20},{5,7},{6,22},{7,5},{8,24},{9,11},... | collective-permute-start | bytes 1400840 | tf_op jit(solution)/shard_map/ppermute | solution.py:83
  96.4 24.5 %collective-permute-start.39 = (bf16[32,7296]{1,0:T(8,128)(2,1)S(1)}, bf16[32,7296]{1,0:T(8,128)(2,1)S(1)}, u32[]{:S(2)}, u32[]{:S(2)}) collective-permute-start(bf16[32,7296]{1,0:T(8,128)(2,1)S(1)} %get-tuple-element.51), channel_id=1, source_target_pairs={{0,16},{1,3},{2,18},{3,1},{4,20},{5,7},{6,22},{7,5},{8,24},{9,11},... | collective-permute-start | bytes 1400840 | tf_op jit(solution)/shard_map/ppermute | solution.py:83
  106.1 15.5 %collective-permute-start.18 = (bf16[32,7168]{1,0:T(8,128)(2,1)S(1)}, bf16[32,7168]{1,0:T(8,128)(2,1)S(1)}, u32[]{:S(2)}, u32[]{:S(2)}) collective-permute-start(bf16[32,7168]{1,0:T(8,128)(2,1)S(1)} %add_convert_fusion.3), channel_id=1, source_target_pairs={{0,2},{1,17},{2,0},{3,19},{4,6},{5,21},{6,4},{7,23},{8,10},{9,25},... | collective-permute-start | bytes 1376264 | tf_op jit(solution)/shard_map/ppermute | solution.py:83
  121.9 10.5 %collective-permute-start.33 = (bf16[8,7168]{1,0:T(8,128)(2,1)S(1)}, bf16[8,7168]{1,0:T(8,128)(2,1)S(1)}, u32[]{:S(2)}, u32[]{:S(2)}) collective-permute-start(bf16[8,7168]{1,0:T(8,128)(2,1)S(1)} %get-tuple-element.57), channel_id=1, source_target_pairs={{0,12},{1,13},{2,14},{3,15},{4,8},{5,9},{6,10},{7,11},{8,4},{9,5},... | collective-permute-start | bytes 344072 | tf_op jit(solution)/shard_map/ppermute | solution.py:83
  124.2 10.3 %collective-permute-start.35 = (bf16[8,7168]{1,0:T(8,128)(2,1)S(1)}, bf16[8,7168]{1,0:T(8,128)(2,1)S(1)}, u32[]{:S(2)}, u32[]{:S(2)}) collective-permute-start(bf16[8,7168]{1,0:T(8,128)(2,1)S(1)} %get-tuple-element.58), channel_id=1, source_target_pairs={{0,4},{1,5},{2,6},{3,7},{4,0},{5,1},{6,2},{7,3},{8,12},{9,13},{10,... | collective-permute-start | bytes 344072 | tf_op jit(solution)/shard_map/ppermute | solution.py:83
  124.2 15.2 %collective-permute-start.34 = (bf16[8,7168]{1,0:T(8,128)(2,1)S(1)}, bf16[8,7168]{1,0:T(8,128)(2,1)S(1)}, u32[]{:S(2)}, u32[]{:S(2)}) collective-permute-start(bf16[8,7168]{1,0:T(8,128)(2,1)S(1)} %get-tuple-element.59), channel_id=1, source_target_pairs={{0,8},{1,9},{2,10},{3,11},{4,12},{5,13},{6,14},{7,15},{8,0},{9,1},... | collective-permute-start | bytes 344072 | tf_op jit(solution)/shard_map/ppermute | solution.py:83
  130.0 10.1 %collective-permute-start.41 = (bf16[8,7296]{1,0:T(8,128)(2,1)S(1)}, bf16[8,7296]{1,0:T(8,128)(2,1)S(1)}, u32[]{:S(2)}, u32[]{:S(2)}) collective-permute-start(bf16[8,7296]{1,0:T(8,128)(2,1)S(1)} %get-tuple-element.54), channel_id=1, source_target_pairs={{0,12},{1,13},{2,14},{3,15},{4,8},{5,9},{6,10},{7,11},{8,4},{9,5},... | collective-permute-start | bytes 350216 | tf_op jit(solution)/shard_map/ppermute | solution.py:83
  132.4 12.4 %collective-permute-start.42 = (bf16[8,7296]{1,0:T(8,128)(2,1)S(1)}, bf16[8,7296]{1,0:T(8,128)(2,1)S(1)}, u32[]{:S(2)}, u32[]{:S(2)}) collective-permute-start(bf16[8,7296]{1,0:T(8,128)(2,1)S(1)} %get-tuple-element.56), channel_id=1, source_target_pairs={{0,8},{1,9},{2,10},{3,11},{4,12},{5,13},{6,14},{7,15},{8,0},{9,1},... | collective-permute-start | bytes 350216 | tf_op jit(solution)/shard_map/ppermute | solution.py:83
  (18 other events, 270.0 us)
